TPU v7x, 32 devices: a whole 2x2x4 slice. The times are simulated.
32 devices in a mesh: grp: 2 (over x), tok: 8 (over z, y), wid: 2 (over core).
Axes of the slice: x: 2, y: 2, z: 4, core: 2. Of those that a mesh axis runs over, the one named last changes fastest.
Arguments:
- inputs: bfloat16 [128, 8192], P(('grp', 'wid'), 'tok'), may hold values from -6 to 6
- parent_gate: bfloat16 [8192, 28672], P('tok', ('grp', 'wid')), may hold values from -0.0625 to 0.0625
- parent_up: bfloat16 [8192, 28672], P('tok', ('grp', 'wid')), may hold values from -0.0625 to 0.0625
- parent_down: bfloat16 [28672, 8192], P(('grp', 'wid'), 'tok'), may hold values from -0.03125 to 0.03125
- first_gate: bfloat16 [8192, 7168], P('tok', ('grp', 'wid')), may hold values from -0.0625 to 0.0625
- first_up: bfloat16 [8192, 7168], P('tok', ('grp', 'wid')), may hold values from -0.0625 to 0.0625
- first_down: bfloat16 [7168, 8192], P(('grp', 'wid'), 'tok'), may hold values from -0.0625 to 0.0625
- second_gate: bfloat16 [8192, 5632], P('tok', ('grp', 'wid')), may hold values from -0.0625 to 0.0625
- second_up: bfloat16 [8192, 5632], P('tok', ('grp', 'wid')), may hold values from -0.0625 to 0.0625
- second_down: bfloat16 [5632, 8192], P(('grp', 'wid'), 'tok'), may hold values from -0.078125 to 0.078125
Outputs:
- target: bfloat16 [128, 8192], P(('grp', 'wid'), 'tok')
- first_error: bfloat16 [128, 8192], P(('grp', 'wid'), 'tok')
- second_error: bfloat16 [128, 8192], P(('grp', 'wid'), 'tok')
- first_grad_gate: bfloat16 [8192, 7168], P('tok', ('grp', 'wid'))
- first_grad_up: bfloat16 [8192, 7168], P('tok', ('grp', 'wid'))
- first_grad_down: bfloat16 [7168, 8192], P(('grp', 'wid'), 'tok')
- second_grad_gate: bfloat16 [8192, 5632], P('tok', ('grp', 'wid'))
- second_grad_up: bfloat16 [8192, 5632], P('tok', ('grp', 'wid'))
- second_grad_down: bfloat16 [5632, 8192], P(('grp', 'wid'), 'tok')
All inputs are finite; a program needn't handle non-finite values.
Results may differ from a plain program's by a relative error of at most 0.009.
Values may be sent and summed in bfloat16 or wider, within the bound.
A program may use at most 192 MiB of HBM per device.

v0:
```python
import functools

import jax
import jax.numpy as jnp
from jax import lax
from jax.experimental import pallas as pl
from jax.experimental.pallas import tpu as pltpu
from jax.sharding import PartitionSpec as P

MESH = pl.DeviceIdType.MESH
LANES = 128
PIECE = 1024
MIB = 1024 * 1024
SLOTS = 4
F32 = jnp.float32
BF16 = jnp.bfloat16


def matmul(left, right):
    return jnp.dot(left, right, preferred_element_type=F32)


def inner_rows(left, right):
    return lax.dot_general(left, right, (((0,), (0,)), ((), ())), preferred_element_type=F32)


def outer_cols(left, right):
    return lax.dot_general(left, right, (((1,), (1,)), ((), ())), preferred_element_type=F32)


def cuts(width):
    units = width // LANES
    count = -(-width // PIECE)
    ranges, at = [], 0
    for i in range(count):
        size = (units // count + (i < units % count)) * LANES
        ranges.append((at, size))
        at += size
    return ranges


def remote(src, dst, send, recv, where):
    return pltpu.make_async_remote_copy(
        src_ref=src, dst_ref=dst, send_sem=send, recv_sem=recv,
        device_id=where, device_id_type=MESH,
    )


def exchange_kernel(grid_of, widths, forward, *refs):
    na, nb = grid_of
    count = len(widths)
    per_in, per_out = (2, 1) if forward else (1, 2)
    refs = list(refs)
    if forward:
        left, weights = refs[0], refs[1:3]
        partial = [refs[-4], refs[-3]] + refs[3:2 * count + 1]
        held, loaded = refs[-2], refs[-1]
        del refs[:2 * count + 1]
        del refs[-4:]
    else:
        partial = refs[:count]
        del refs[:count]
    if forward:
        gathered = refs[:count]
        share = refs[count:3 * count]
        del refs[:3 * count]
    else:
        share = refs[:2 * count]
        gathered = refs[2 * count:4 * count]
        del refs[:4 * count]
    got1, sum1, got2, s1, r1, s2, r2, s3, r3, s4, r4 = refs

    me = lax.axis_index("tok")
    hi, lo = me // nb, lax.rem(me, nb)
    hi_peers = [lax.rem(hi + d, na) for d in range(1, na)]
    lo_peers = [lax.rem(lo + d, nb) for d in range(1, nb)]

    jobs, at = [], 0
    order = list(range(1, count)) + [0] if forward else list(range(count))
    for k in order:
        for start, size in cuts(widths[k]):
            jobs.append((k, start, size, at))
            at += size * per_in
    made = [j for j, job in enumerate(jobs) if forward and job[0] == 0]

    def load(n):
        k, start, size, col = jobs[made[n]]
        return [
            pltpu.make_async_copy(
                weights[i].at[:, pl.ds(start, size)],
                held.at[n % SLOTS, i, :, pl.ds(0, size)],
                loaded.at[n % SLOTS, i],
            )
            for i in range(2)
        ]

    for n in range(min(SLOTS, len(made))):
        for copy in load(n):
            copy.start()

    barrier = pltpu.get_barrier_semaphore()
    for peer in hi_peers:
        pl.semaphore_signal(barrier, inc=1, device_id={"tok": peer * nb + lo}, device_id_type=MESH)
    for peer in lo_peers:
        pl.semaphore_signal(barrier, inc=1, device_id={"tok": hi * nb + peer}, device_id_type=MESH)
    pl.semaphore_wait(barrier, na + nb - 2)

    pending = []
    first, second, third, fourth = {}, {}, {}, {}

    def send_low(j):
        k, start, size, col = jobs[j]
        if j in made:
            n = made.index(j)
            for i, copy in enumerate(load(n)):
                copy.wait()
                product = matmul(left[...], held[n % SLOTS, i, :, pl.ds(0, size)]).astype(BF16)
                partial[i][:, :, :, pl.ds(start, size)] = product.reshape(
                    na, nb, left.shape[0] // (na * nb), size
                )
            if n + SLOTS < len(made):
                for copy in load(n + SLOTS):
                    copy.start()
        first[j] = []
        for d, peer in enumerate(lo_peers):
            for i in range(per_in):
                copy = remote(
                    partial[per_in * k + i].at[:, peer, :, pl.ds(start, size)],
                    got1.at[d, :, :, pl.ds(col + i * size, size)],
                    s1.at[j, d, i], r1.at[j, d, i], {"tok": hi * nb + peer},
                )
                copy.start()
                first[j].append(copy)
        pending.extend(first[j])

    def add_low(j):
        k, start, size, col = jobs[j]
        for copy in first[j]:
            copy.wait_recv()
        for i in range(per_in):
            cols = pl.ds(col + i * size, size)
            total = partial[per_in * k + i][:, lo, :, pl.ds(start, size)].astype(F32)
            for d in range(nb - 1):
                total = total + got1[d, :, :, cols].astype(F32)
            sum1[:, :, cols] = total.astype(BF16)
        second[j] = []
        cols = pl.ds(col, size * per_in)
        for d, peer in enumerate(hi_peers):
            copy = remote(
                sum1.at[peer, :, cols], got2.at[d, :, cols], s2.at[j, d], r2.at[j, d],
                {"tok": peer * nb + lo},
            )
            copy.start()
            second[j].append(copy)
        pending.extend(second[j])

    def add_high(j):
        k, start, size, col = jobs[j]
        for copy in second[j]:
            copy.wait_recv()
        totals = []
        for i in range(per_in):
            cols = pl.ds(col + i * size, size)
            total = partial[per_in * k + i][hi, lo, :, pl.ds(start, size)].astype(F32)
            for d in range(nb - 1):
                total = total + got1[d, hi, :, cols].astype(F32)
            for d in range(na - 1):
                total = total + got2[d, :, cols].astype(F32)
            totals.append(total)
        window = pl.ds(start, size)
        if forward:
            gate, up = totals
            share[2 * k][:, window] = gate
            share[2 * k + 1][:, window] = up
            gathered[k][hi, lo, :, window] = (gate / (1.0 + jnp.exp(-gate)) * up).astype(BF16)
            outs = [gathered[k]]
        else:
            back = totals[0]
            gate = share[2 * k][:, window]
            up = share[2 * k + 1][:, window]
            s = 1.0 / (1.0 + jnp.exp(-gate))
            outs = [gathered[2 * k], gathered[2 * k + 1]]
            outs[0][hi, lo, :, window] = (back * up * s * (1.0 + gate * (1.0 - s))).astype(BF16)
            outs[1][hi, lo, :, window] = (back * gate * s).astype(BF16)
        third[j] = []
        for d, peer in enumerate(hi_peers):
            for i, out in enumerate(outs):
                here = out.at[hi, lo, :, window]
                copy = remote(
                    here, here, s3.at[j, d, i], r3.at[j, d, i], {"tok": peer * nb + lo}
                )
                copy.start()
                third[j].append(copy)
        pending.extend(third[j])

    def spread_low(j):
        k, start, size, col = jobs[j]
        for copy in third[j]:
            copy.wait_recv()
        outs = [gathered[per_out * k + i] for i in range(per_out)]
        fourth[j] = []
        for d, peer in enumerate(lo_peers):
            for i, out in enumerate(outs):
                here = out.at[:, lo, :, pl.ds(start, size)]
                copy = remote(
                    here, here, s4.at[j, d, i], r4.at[j, d, i], {"tok": hi * nb + peer}
                )
                copy.start()
                fourth[j].append(copy)
        pending.extend(fourth[j])

    total_jobs = len(jobs)
    ahead = total_jobs - len(made) + 1 if made else total_jobs
    for j in range(min(ahead, total_jobs)):
        send_low(j)
    for step in range(total_jobs + 2):
        if step + ahead < total_jobs:
            send_low(step + ahead)
        if step < total_jobs:
            add_low(step)
        if 0 <= step - 1 < total_jobs:
            add_high(step - 1)
        if 0 <= step - 2 < total_jobs:
            spread_low(step - 2)
    for j in range(total_jobs):
        for copy in fourth[j]:
            copy.wait_recv()
    for copy in pending:
        copy.wait_send()


def padded(x):
    return jnp.pad(x, ((0, 0), (0, -x.shape[1] % LANES)))


def exchange(arrays, shares, tok, forward, ident, product=()):
    na = 4 if tok % 4 == 0 else 1
    nb = tok // na
    per_in, per_out = (2, 1) if forward else (1, 2)
    tokens = arrays[0].shape[0]
    rows = tokens // tok
    real = [x.shape[1] for x in tuple(product[1:]) + tuple(arrays)]
    product = list(product[:1]) + [padded(x) for x in product[1:]]
    arrays = [padded(x) for x in arrays]
    all_widths = [x.shape[1] for x in product[1:] + arrays]
    widths = all_widths[::per_in]
    count = len(widths)
    all_cols = per_in * sum(widths)
    n_jobs = sum(len(cuts(w)) for w in widths)
    gathered = [
        jax.ShapeDtypeStruct((na, nb, rows, w), BF16) for w in widths for _ in range(per_out)
    ]
    kept = [jax.ShapeDtypeStruct((rows, w), F32) for w in widths for _ in range(2)]
    lead = max(nb - 1, 1)
    dma = pltpu.SemaphoreType.DMA
    scratch = [
        pltpu.VMEM((lead, na, rows, all_cols), BF16),
        pltpu.VMEM((na, rows, all_cols), BF16),
        pltpu.VMEM((max(na - 1, 1), rows, all_cols), BF16),
        dma((n_jobs, lead, per_in)), dma((n_jobs, lead, per_in)),
        dma((n_jobs, max(na - 1, 1))), dma((n_jobs, max(na - 1, 1))),
        dma((n_jobs, max(na - 1, 1), per_out)), dma((n_jobs, max(na - 1, 1), per_out)),
        dma((n_jobs, lead, per_out)), dma((n_jobs, lead, per_out)),
    ]
    outs = gathered + kept if forward else gathered
    vmem = pl.BlockSpec(memory_space=pltpu.VMEM)
    in_specs = [vmem] * (len(arrays) + len(shares))
    if forward:
        piece = max(size for _, size in cuts(widths[0]))
        scratch += [pltpu.VMEM((na, nb, rows, widths[0]), BF16)] * 2
        scratch += [
            pltpu.VMEM((SLOTS, 2, product[0].shape[1], piece), BF16), dma((SLOTS, 2)),
        ]
        in_specs = [vmem] + [pl.BlockSpec(memory_space=pl.ANY)] * 2 + in_specs
    operands = product + [x.reshape(na, nb, rows, x.shape[1]) for x in arrays] + list(shares)
    results = pl.pallas_call(
        functools.partial(exchange_kernel, (na, nb), widths, forward),
        out_shape=outs,
        in_specs=in_specs,
        out_specs=[vmem] * len(outs),
        scratch_shapes=scratch,
        compiler_params=pltpu.CompilerParams(
            collective_id=ident, has_side_effects=True,
            vmem_limit_bytes=(36 if forward else 10) * MIB,
        ),
        name="forward_exchange" if forward else "backward_exchange",
    )(*operands)
    full = [
        x.reshape(tokens, x.shape[-1])[:, : real[i * per_in // per_out]]
        for i, x in enumerate(results[: len(gathered)])
    ]
    return full, results[len(gathered):]


def hidden_group(sizes):
    ngrp, nwid = sizes
    total = ngrp * nwid
    me = lax.axis_index("grp") * nwid + lax.axis_index("wid")
    peers = [lax.rem(me + d, total) for d in range(1, total)]
    places = [{"grp": p // nwid, "wid": lax.rem(p, nwid)} for p in peers]
    barrier = pltpu.get_barrier_semaphore()
    for place in places:
        pl.semaphore_signal(barrier, inc=1, device_id=place, device_id_type=MESH)
    pl.semaphore_wait(barrier, total - 1)
    return me, peers, places


def gather_kernel(sizes, x_ref, out_ref, own, send, recv):
    me, peers, places = hidden_group(sizes)
    copies = []
    for d, place in enumerate(places):
        copy = remote(x_ref, out_ref.at[me], send.at[d], recv.at[d], place)
        copy.start()
        copies.append(copy)
    local = pltpu.make_async_copy(x_ref, out_ref.at[me], own)
    local.start()
    local.wait()
    for copy in copies:
        copy.wait()


def gather_rows(x, sizes):
    total = sizes[0] * sizes[1]
    vmem = pl.BlockSpec(memory_space=pltpu.VMEM)
    dma = pltpu.SemaphoreType.DMA
    out = pl.pallas_call(
        functools.partial(gather_kernel, sizes),
        out_shape=jax.ShapeDtypeStruct((total,) + x.shape, x.dtype),
        in_specs=[vmem],
        out_specs=vmem,
        scratch_shapes=[dma, dma((total - 1,)), dma((total - 1,))],
        compiler_params=pltpu.CompilerParams(
            collective_id=0, has_side_effects=True, vmem_limit_bytes=4 * MIB
        ),
        name="gather_rows",
    )(x)
    return out.reshape(total * x.shape[0], x.shape[1])


def down_step(features):
    return 256 if features % 256 == 0 else features


def errors_kernel(
    sizes, hidden, down, a_ref, b_ref, target, a_err, b_err, a_all, b_all, t_ref, got,
    s1, r1, s2, r2, s3, r3,
):
    me, peers, places = hidden_group(sizes)
    sources = (t_ref, a_ref, b_ref)
    copies = []
    for i in (1, 2):
        for d, (peer, place) in enumerate(zip(peers, places)):
            copy = remote(sources[i].at[peer], got.at[d, i], s1.at[d, i], r1.at[d, i], place)
            copy.start()
            copies.append(copy)
    total, rows, features = t_ref.shape
    step = down_step(features)
    for c in range(features // step):
        cols = pl.ds(c * step, step)
        part = matmul(hidden[...], down[:, cols])
        t_ref[:, :, cols] = part.astype(BF16).reshape(total, rows, step)
        for d, (peer, place) in enumerate(zip(peers, places)):
            copy = remote(
                t_ref.at[peer, :, cols], got.at[d, 0, :, cols], s3.at[d, c], r3.at[d, c], place
            )
            copy.start()
            copies.append(copy)
    for copy in copies:
        copy.wait_recv()
    totals = []
    for i, source in enumerate(sources):
        total = source[me].astype(F32)
        for d in range(len(peers)):
            total = total + got[d, i].astype(F32)
        totals.append(total)
    goal = totals[0].astype(BF16)
    target[...] = goal
    goal = goal.astype(F32)
    sends = []
    for i, (total, own, full) in enumerate(
        ((totals[1], a_err, a_all), (totals[2], b_err, b_all))
    ):
        value = (total - goal).astype(BF16)
        own[...] = value
        full[me] = value
        for d, place in enumerate(places):
            copy = remote(full.at[me], full.at[me], s2.at[d, i], r2.at[d, i], place)
            copy.start()
            sends.append(copy)
    for copy in sends:
        copy.wait_recv()
    for copy in copies + sends:
        copy.wait_send()


def errors(hidden, down, parts, sizes):
    total = sizes[0] * sizes[1]
    tokens, features = parts[0].shape
    pieces = features // down_step(features)
    rows = tokens // total
    vmem = pl.BlockSpec(memory_space=pltpu.VMEM)
    dma = pltpu.SemaphoreType.DMA
    own = jax.ShapeDtypeStruct((rows, features), BF16)
    full = jax.ShapeDtypeStruct((total, rows, features), BF16)
    target, a_err, b_err, a_all, b_all = pl.pallas_call(
        functools.partial(errors_kernel, sizes),
        out_shape=[own, own, own, full, full],
        in_specs=[vmem] * 4,
        out_specs=[vmem] * 5,
        scratch_shapes=[
            pltpu.VMEM((total, rows, features), BF16),
            pltpu.VMEM((total - 1, 3, rows, features), BF16),
            dma((total - 1, 3)), dma((total - 1, 3)), dma((total - 1, 2)), dma((total - 1, 2)),
            dma((total - 1, pieces)), dma((total - 1, pieces)),
        ],
        compiler_params=pltpu.CompilerParams(
            collective_id=1, has_side_effects=True, vmem_limit_bytes=24 * MIB
        ),
        name="errors",
    )(hidden, down, *[x.reshape(total, rows, features) for x in parts])
    return target, a_err, b_err, a_all.reshape(tokens, -1), b_all.reshape(tokens, -1)


def outer_kernel(columns, *refs):
    half = len(refs) // 2
    left = columns[...].T
    for grad, out in zip(refs[:half], refs[half:]):
        out[...] = matmul(left, grad[...]).astype(BF16)


def weight_grads(columns, grads):
    tokens, features = columns.shape
    tile = LANES
    out_bytes = 2 * features * sum(g.shape[1] for g in grads)
    return pl.pallas_call(
        outer_kernel,
        grid=(features // tile,),
        out_shape=[jax.ShapeDtypeStruct((features, g.shape[1]), BF16) for g in grads],
        in_specs=[pl.BlockSpec((tokens, tile), lambda i: (0, i))]
        + [pl.BlockSpec(memory_space=pltpu.VMEM)] * len(grads),
        out_specs=[pl.BlockSpec((tile, g.shape[1]), lambda i: (i, 0)) for g in grads],
        compiler_params=pltpu.CompilerParams(vmem_limit_bytes=16 * MIB),
        cost_estimate=pl.CostEstimate(
            flops=tokens * out_bytes, bytes_accessed=out_bytes, transcendentals=0
        ),
        name="weight_grads",
    )(columns, *grads)


def body(
    tok, sizes, inputs, parent_gate, parent_up, parent_down, first_gate, first_up, first_down,
    second_gate, second_up, second_down,
):
    columns = gather_rows(inputs, sizes)
    weights = (first_gate, first_up, second_gate, second_up)
    partials = [matmul(columns, w).astype(BF16) for w in weights]
    (parent_hidden, first_hidden, second_hidden), kept = exchange(
        partials, (), tok, True, 2, (columns, parent_gate, parent_up)
    )
    outs = [
        matmul(first_hidden, first_down).astype(BF16),
        matmul(second_hidden, second_down).astype(BF16),
    ]
    target, first_error, second_error, first_all, second_all = errors(
        parent_hidden, parent_down, outs, sizes
    )
    backs = [
        outer_cols(first_all, first_down).astype(BF16),
        outer_cols(second_all, second_down).astype(BF16),
    ]
    grads, _ = exchange(backs, kept[2:], tok, False, 3)
    first_grad_down = inner_rows(first_hidden, first_all).astype(BF16)
    second_grad_down = inner_rows(second_hidden, second_all).astype(BF16)
    first_grad_gate, first_grad_up, second_grad_gate, second_grad_up = weight_grads(
        columns, grads
    )
    return (
        target, first_error, second_error,
        first_grad_gate, first_grad_up, first_grad_down,
        second_grad_gate, second_grad_up, second_grad_down,
    )


def solution(mesh):
    tok = mesh.shape["tok"]
    sizes = (mesh.shape["grp"], mesh.shape["wid"])
    rows = P(("grp", "wid"), "tok")
    cols = P("tok", ("grp", "wid"))
    return jax.shard_map(
        functools.partial(body, tok, sizes),
        mesh=mesh,
        in_specs=(rows, cols, cols, rows, cols, cols, rows, cols, cols, rows),
        out_specs=(rows, rows, rows, cols, cols, rows, cols, cols, rows),
        check_vma=False,
    )
```

profile of v0, /device:TPU:0, one launch (start us, length us, event | category | flops | bytes accessed | tf_op | source)
XLA Modules:
  0.0 197.3 jit_solution(2166800906027438357)
XLA Ops:
  0.6 0.0 copy-start
  0.7 0.0 copy-start.1
  0.7 1.0 copy-done.1
  1.6 0.0 copy-start.3
  1.6 6.3 %gather_rows.1 = bf16[4,32,1024]{2,1,0:T(8,128)(2,1)S(1)} custom-call(bf16[32,1024]{1,0:T(8,128)(2,1)S(1)} %copy-done.1), custom_call_target="tpu_custom_call" | custom-call | tf_op jit(solution)/shard_map/gather_rows/pallas_call | solution.py:326
  8.0 0.0 copy-start.4
  8.0 2.8 %convolution_convert_fusion.4 = bf16[128,1792]{1,0:T(8,128)(2,1)S(1)} fusion(bf16[128,1024]{1,0:T(8,128)(2,1)S(1)} %bitcast.40, bf16[1024,1792]{1,0:T(8,128)(2,1)} %param.14), kind=kOutput, calls=%fused_computation.4 | convolution fusion | flops 469991424 | bytes 4390912 | tf_op jit(solution)/shard_map/dot_general | solution.py:20
  10.9 0.0 copy-done.3
  10.9 0.0 copy-start.5
  10.9 0.7 convolution_convert_fusion.3
  11.5 0.0 copy-done.4
  11.6 0.6 convolution_convert_fusion.7
  12.2 0.6 copy-done.5
  12.7 0.6 convolution_convert_fusion.6
  13.3 0.0 slice-start
  13.3 0.0 copy-start.2
  13.3 0.0 slice-start.1
  13.3 0.0 slice-start.2
  13.3 0.0 slice-start.3
  13.4 106.2 %forward_exchange.1 = (bf16[4,2,16,7168]{3,2,1,0:T(8,128)(2,1)S(1)}, bf16[4,2,16,1792]{3,2,1,0:T(8,128)(2,1)S(1)}, bf16[4,2,16,1408]{3,2,1,0:T(8,128)(2,1)S(1)},...) custom-call(bf16[128,1024]{1,0:T(8,128)(2,1)S(1)} %bitcast.44, ...), custom_call_target="tpu_custom_call" | custom-call | tf_op jit(solution)/shard_map/forward_exchange/pallas_call | solution.py:276
  119.6 0.0 copy-done.2
  119.6 0.6 convolution_convert_fusion.8
  120.2 0.0 copy-done
  120.2 0.6 convolution_convert_fusion.9
  120.8 0.0 slice-done
  120.8 0.0 slice-done.1
  120.8 0.0 slice-done.2
  120.8 0.0 slice-done.3
  120.9 19.5 %errors.1 = (bf16[32,1024]{1,0:T(8,128)(2,1)S(1)}, bf16[32,1024]{1,0:T(8,128)(2,1)S(1)}, bf16[32,1024]{1,0:T(8,128)(2,1)S(1)}, bf16[4,32,1024]{2,1,0:T(8,128)(2,1)S(1)}, bf16[4,32,1024]{2,1,0:T(8,128)(2,1)S(1)}) custom-call(bf16[128,7168]{1,0:T(8,128)(2,1)S(1)} %bitcast.50, bf16[7168,1024]{1,0:T(8,128)(2,1)S(1)} %bitcast.39, ...), custom_call_target="tpu_custom_call" | custom-call | tf_op jit(solution)/shard_map/errors/pallas_call | solution.py:405
  140.4 1.3 convolution_convert_fusion.2
  141.7 1.0 convolution_convert_fusion.5
  142.8 40.1 %backward_exchange.1 = (bf16[4,2,16,1792]{3,2,1,0:T(8,128)(2,1)S(1)}, bf16[4,2,16,1792]{3,2,1,0:T(8,128)(2,1)S(1)}, bf16[4,2,16,1408]{3,2,1,0:T(8,128)(2,1)S(1)}, bf16[4,2,16,1408]{3,2,1,0:T(8,128)(2,1)S(1)}) custom-call(bf16[4,2,16,1792]{3,2,1,0:T(8,128)(2,1)S(1)} %bitcast.51, bf16[4,2,16,1408]{3,2,1,0:T(8,128)(2,1)S(1)} %bitcast.52, ...), custom_call_target="tpu_custom_call" | custom-call | tf_op jit(solution)/shard_map/backward_exchange/pallas_call | solution.py:276
  182.9 7.0 %weight_grads.1 = (bf16[1024,1792]{1,0:T(8,128)(2,1)}, bf16[1024,1792]{1,0:T(8,128)(2,1)}, bf16[1024,1408]{1,0:T(8,128)(2,1)}, bf16[1024,1408]{1,0:T(8,128)(2,1)}) custom-call(bf16[128,1024]{1,0:T(8,128)(2,1)S(1)} %bitcast.45, bf16[128,1792]{1,0:T(8,128)(2,1)S(1)} %bitcast.63, bf16[128,1792]{1,0:T(8,128)(2,1)S(1)} %bitcast.64, ...), custom_call_target="tpu_custom_call" | custom-call | flops 1677721600 | bytes 13107200 | tf_op jit(solution)/shard_map/weight_grads/pallas_call | solution.py:435
  189.9 3.0 %convolution_convert_fusion.1 = bf16[1792,1024]{1,0:T(8,128)(2,1)} fusion(bf16[128,1792]{1,0:T(8,128)(2,1)S(1)} %bitcast.47, bf16[128,1024]{1,0:T(8,128)(2,1)S(1)} %bitcast.60), kind=kOutput, calls=%fused_computation.1 | convolution fusion | flops 471597056 | bytes 4390912 | tf_op jit(solution)/shard_map/dot_general | solution.py:24
  192.9 2.5 %convolution_convert_fusion = bf16[1408,1024]{1,0:T(8,128)(2,1)} fusion(bf16[128,1408]{1,0:T(8,128)(2,1)S(1)} %bitcast.54, bf16[128,1024]{1,0:T(8,128)(2,1)S(1)} %bitcast.62), kind=kOutput, calls=%fused_computation | convolution fusion | flops 370540544 | bytes 3506176 | tf_op jit(solution)/shard_map/dot_general | solution.py:24
  195.4 0.6 copy.22
  196.0 0.6 copy.23
  196.7 0.6 copy.24
  (1 shorter events, 0.0 us)
Async XLA Ops:
  0.6 119.6 %copy-start = (bf16[1408,1024]{1,0:T(8,128)(2,1)S(1)}, bf16[1408,1024]{1,0:T(8,128)(2,1)}, u32[]{:S(2)}) copy-start(bf16[1408,1024]{1,0:T(8,128)(2,1)} %param.19) | copy-start | bytes 8650756
  0.7 1.0 copy-start.1
  1.6 9.2 %copy-start.3 = (bf16[1024,1792]{1,0:T(8,128)(2,1)S(1)}, bf16[1024,1792]{1,0:T(8,128)(2,1)}, u32[]{:S(2)}) copy-start(bf16[1024,1792]{1,0:T(8,128)(2,1)} %param.15) | copy-start | bytes 11010052
  8.0 3.5 %copy-start.4 = (bf16[1024,1408]{1,0:T(8,128)(2,1)S(1)}, bf16[1024,1408]{1,0:T(8,128)(2,1)}, u32[]{:S(2)}) copy-start(bf16[1024,1408]{1,0:T(8,128)(2,1)} %param.17) | copy-start | bytes 8650756
  10.9 1.8 copy-start.5
  13.3 107.5 %slice-start = ((s8[14680064]{0:T(1024)(128)(4,1)}), s8[4194304]{0:T(1024)(128)(4,1)S(1)}, s32[]{:S(2)}) async-start(s8[14680064]{0:T(1024)(128)(4,1)} %bitcast.38), calls=%async_computation | async-start | bytes 8388608
  13.3 106.2 %copy-start.2 = (bf16[1792,1024]{1,0:T(8,128)(2,1)S(1)}, bf16[1792,1024]{1,0:T(8,128)(2,1)}, u32[]{:S(2)}) copy-start(bf16[1792,1024]{1,0:T(8,128)(2,1)} %param.16) | copy-start | bytes 11010052
  13.3 107.5 %slice-start.1 = ((s8[14680064]{0:T(1024)(128)(4,1)}), s8[4194304]{0:T(1024)(128)(4,1)S(1)}, s32[]{:S(2)}) async-start(s8[14680064]{0:T(1024)(128)(4,1)} %bitcast.38), calls=%async_computation.1 | async-start | bytes 8388608
  13.3 107.5 %slice-start.2 = ((s8[14680064]{0:T(1024)(128)(4,1)}), s8[4194304]{0:T(1024)(128)(4,1)S(1)}, s32[]{:S(2)}) async-start(s8[14680064]{0:T(1024)(128)(4,1)} %bitcast.38), calls=%async_computation.2 | async-start | bytes 8388608
  13.3 107.5 %slice-start.3 = ((s8[14680064]{0:T(1024)(128)(4,1)}), s8[2097152]{0:T(1024)(128)(4,1)S(1)}, s32[]{:S(2)}) async-start(s8[14680064]{0:T(1024)(128)(4,1)} %bitcast.38), calls=%async_computation.3 | async-start | bytes 4194304
where the time goes:
time: 197 us
  Pallas kernels  179 us (91%)
  matrix products  13.8 us (7%)
  local copies, waits for them, and re-layouts  3.47 us (2%)
    pallas_call x2, Pallas kernels, exchange(): pl.pallas_call(functools.partial(exchange_kernel, (na, nb), widths, forwa...  146 us
    pallas_call x1, Pallas kernels, errors(): pl.pallas_call(functools.partial(errors_kernel, sizes), out_shape=[own, o...  19.5 us
    pallas_call x1, Pallas kernels, weight_grads(): pl.pallas_call(outer_kernel, grid=(features // tile,), out_shape=[jax.Sha...  6.96 us
    pallas_call x1, Pallas kernels, gather_rows(): pl.pallas_call(functools.partial(gather_kernel, sizes), out_shape=jax.Sha...  6.35 us
    dot_general x6, matrix products, matmul(): return jnp.dot(left, right, preferred_element_type=F32)  5.9 us
    dot_general x2, matrix products, inner_rows(): lax.dot_general(left, right, (((0,), (0,)), ((), ())), preferred_element_...  5.49 us

commit v1 on v0

v1 whole, which is shorter than its diff:
```python
import functools

import jax
import jax.numpy as jnp
from jax import lax
from jax.experimental import pallas as pl
from jax.experimental.pallas import tpu as pltpu
from jax.sharding import PartitionSpec as P

MESH = pl.DeviceIdType.MESH
LANES = 128
MIB = 1024 * 1024
SLOTS = 4
FORWARD_STEPS = (2, 2, 2, 1, 2, 2, 2)
BACKWARD_STEPS = (3, 3, 3, 3, 4, 3, 2)
FORWARD_MIB = 48
F32 = jnp.float32
BF16 = jnp.bfloat16


def matmul(left, right):
    return jnp.dot(left, right, preferred_element_type=F32)


def inner_rows(left, right):
    return lax.dot_general(left, right, (((0,), (0,)), ((), ())), preferred_element_type=F32)


def outer_cols(left, right):
    return lax.dot_general(left, right, (((1,), (1,)), ((), ())), preferred_element_type=F32)


def remote(src, dst, send, recv, where):
    return pltpu.make_async_remote_copy(
        src_ref=src, dst_ref=dst, send_sem=send, recv_sem=recv,
        device_id=where, device_id_type=MESH,
    )


def divisor(total, most):
    return max(k for k in range(1, most + 1) if total % k == 0)


def relay(dims, steps, produce, finish, consume, partial, out, span, bufs, sems, prepare):
    na, nb, jobs, slots = dims
    side = nb - 1
    ay_out, ay_in, az_out, az_in, bz_out, bz_in, by_out, by_in = bufs
    (say, ray, saz, raz, sbz, rbz, sby, rby,
     tay, uay, taz, uaz, tbz, ubz, tby, uby) = sems

    me = lax.axis_index("tok")
    hi, lo = me // nb, lax.rem(me, nb)
    peers = [lax.rem(lo + d, nb) for d in range(1, nb)]
    beside = [{"tok": hi * nb + p} for p in peers]
    pos = [hi, na - 1 - hi]
    far = [na - 1 - p for p in pos]
    onward = [
        {"tok": lax.rem(hi + 1, na) * nb + lo}, {"tok": lax.rem(hi + na - 1, na) * nb + lo}
    ]
    back = onward[::-1]
    end = (hi == 0) | (hi == na - 1)
    turn = jnp.where(hi == na - 1, 0, 1)

    barrier = pltpu.get_barrier_semaphore()
    for where in beside:
        pl.semaphore_signal(barrier, inc=1, device_id=where, device_id_type=MESH)
    for d in range(2):
        @pl.when(pos[d] < na - 1)
        def _(d=d):
            pl.semaphore_signal(barrier, inc=1, device_id=onward[d], device_id_type=MESH)
    prepare(barrier, side + jnp.where(end, 1, 2))

    def a_block(y, d):
        return y * 2 + d

    def b_block(y, d):
        return 2 * nb + d * nb + y

    def piece(block, j, count=1):
        return out.at[pl.ds(block, count), :, pl.ds(pl.multiple_of(j * span, LANES), span)]

    def copy_ay(j, k):
        return remote(ay_out.at[j, k], ay_in.at[j, k], say.at[j, k], ray.at[j, k], beside[k])

    def copy_az(j, d):
        return remote(az_out.at[j, d], az_in.at[j, d], saz.at[j, d], raz.at[j, d], onward[d])

    def copy_bz(j, d):
        return remote(bz_out.at[j, d], bz_in.at[j, d], sbz.at[j, d], rbz.at[j, d], onward[d])

    def copy_by(j, k):
        return remote(by_out.at[j, k], by_in.at[j, k], sby.at[j, k], rby.at[j, k], beside[k])

    def spread_az(j, d):
        here = piece(a_block(lo, d), j)
        return remote(here, here, taz.at[j, d], uaz.at[j, d], back[d])

    def spread_ay(j, d, k):
        here = piece(a_block(lo, d), j)
        return remote(here, here, tay.at[j, d, k], uay.at[j, d, k], beside[k])

    def spread_by(j, k):
        here = piece(b_block(lo, turn), j)
        return remote(here, here, tby.at[j, k], uby.at[j, k], beside[k])

    def spread_bz(j, d):
        here = piece(b_block(0, d), j, nb)
        return remote(here, here, tbz.at[j, d], ubz.at[j, d], back[d])

    def on(j, condition=None):
        inside = (j >= 0) & (j < jobs)
        return pl.when(inside if condition is None else inside & condition)

    def begin(j):
        slot = lax.rem(j, slots)
        produce(j, slot)
        for k in range(side):
            ay_out[j, k] = partial[slot, pl.ds(peers[k] * 2, 2)].astype(BF16)
            copy_ay(j, k).start()
        for d in range(2):
            @pl.when(pos[d] == 0)
            def _(d=d):
                bz_out[j, d] = partial[slot, pl.ds(b_block(0, d), nb)].astype(BF16)
                copy_bz(j, d).start()

    def pair(j):
        slot = lax.rem(j, slots)
        for k in range(side):
            copy_ay(j, k).wait_recv()
        for d in range(2):
            total = partial[slot, a_block(lo, d)]
            for k in range(side):
                total = total + ay_in[j, k, d].astype(F32)
            partial[slot, a_block(lo, d)] = total

            @pl.when(pos[d] == 0)
            def _(d=d, total=total):
                az_out[j, d] = total.astype(BF16)
                copy_az(j, d).start()

    def along_a(j, d):
        slot = lax.rem(j, slots)
        copy_az(j, d).wait_recv()
        total = partial[slot, a_block(lo, d)] + az_in[j, d].astype(F32)

        @pl.when(pos[d] < na - 1)
        def _():
            az_out[j, d] = total.astype(BF16)
            copy_az(j, d).start()

        @pl.when(pos[d] == na - 1)
        def _():
            finish(j, 0, a_block(lo, d), total)
            spread_az(j, d).start()
            for k in range(side):
                spread_ay(j, d, k).start()

    def along_b(j, d):
        slot = lax.rem(j, slots)
        copy_bz(j, d).wait_recv()

        @pl.when(pos[d] < na - 1)
        def _():
            for y in range(nb):
                total = partial[slot, b_block(y, d)] + bz_in[j, d, y].astype(F32)
                bz_out[j, d, y] = total.astype(BF16)
            copy_bz(j, d).start()

        @pl.when(pos[d] == na - 1)
        def _():
            for k in range(side):
                total = partial[slot, b_block(peers[k], d)]
                total = total + bz_in[j, d, peers[k]].astype(F32)
                by_out[j, k] = total.astype(BF16)
                copy_by(j, k).start()
            total = partial[slot, b_block(lo, d)] + bz_in[j, d, lo].astype(F32)
            partial[slot, b_block(lo, d)] = total

    def corner(j):
        slot = lax.rem(j, slots)
        block = b_block(lo, turn)
        total = partial[slot, block]
        for k in range(side):
            copy_by(j, k).wait_recv()
            total = total + by_in[j, k].astype(F32)
        finish(j, 1, block, total)
        for k in range(side):
            spread_by(j, k).start()

    def leave_b(j):
        for k in range(side):
            spread_by(j, k).wait_recv()
        for d in range(2):
            @pl.when(pos[d] == na - 1)
            def _(d=d):
                spread_bz(j, d).start()

    def pass_a(j, d):
        spread_az(j, d).wait_recv()

        @pl.when(far[d] < na - 1)
        def _():
            spread_az(j, d).start()

        for k in range(side):
            spread_ay(j, d, k).start()

    def pass_b(j, d):
        spread_bz(j, d).wait_recv()

        @pl.when(far[d] < na - 1)
        def _():
            spread_bz(j, d).start()

    start_a, walk_a, walk_b, turn_b, turn_c, open_a, open_b = steps
    top = start_a + walk_a * (na - 1)
    turn_at = walk_b * (na - 1) + turn_b
    leave_at = turn_at + turn_c
    done = 1 + max(top + open_a * na, leave_at + open_b * (na - 1))

    def tick(t, carry):
        on(t)(functools.partial(begin, t))
        j = t - start_a
        on(j)(functools.partial(pair, j))
        for d in range(2):
            j = t - walk_b * pos[d]
            on(j, pos[d] > 0)(functools.partial(along_b, j, d))
        for d in range(2):
            j = t - start_a - walk_a * pos[d]
            on(j, pos[d] > 0)(functools.partial(along_a, j, d))
        j = t - turn_at
        on(j, end)(functools.partial(corner, j))
        j = t - leave_at
        on(j, end)(functools.partial(leave_b, j))
        for d in range(2):
            j = t - top - open_a * far[d]
            on(j, far[d] > 0)(functools.partial(pass_a, j, d))
        for d in range(2):
            j = t - leave_at - open_b * far[d]
            on(j, far[d] > 0)(functools.partial(pass_b, j, d))
        j = t - done
        on(j)(functools.partial(arrive, j))
        return carry

    def arrive(j):
        for k in range(side):
            for d in range(2):
                spread_ay(j, d, k).wait_recv()
        consume(j)

    lax.fori_loop(0, jobs + done, tick, 0)

    def drain(j, carry):
        for k in range(side):
            copy_ay(j, k).wait_send()
            for d in range(2):
                spread_ay(j, d, k).wait_send()
        for d in range(2):
            @pl.when(pos[d] < na - 1)
            def _(d=d):
                copy_az(j, d).wait_send()
                copy_bz(j, d).wait_send()

            @pl.when(far[d] < na - 1)
            def _(d=d):
                spread_az(j, d).wait_send()
                spread_bz(j, d).wait_send()

        @pl.when(end)
        def _():
            for k in range(side):
                copy_by(j, k).wait_send()
                spread_by(j, k).wait_send()

        return carry

    return lambda: lax.fori_loop(0, jobs, drain, 0)


def relay_scratch(dims, rows, width):
    na, nb, jobs, slots = dims
    side = max(nb - 1, 1)
    dma = pltpu.SemaphoreType.DMA

    def room(*shape):
        return pltpu.VMEM((jobs,) + shape + (rows, width), BF16)

    bufs = [
        room(side, 2), room(side, 2), room(2), room(2),
        room(2, nb), room(2, nb), room(side), room(side),
    ]
    counts = [(side,), (2,), (2,), (side,), (2, side), (2,), (2,), (side,)]
    sems = [dma((jobs,) + c) for c in counts for _ in range(2)]
    partial = pltpu.VMEM((slots, 4 * nb, rows, width), F32)
    return [partial] + bufs + sems


def ring_slots(na, steps):
    return 1 + max(steps[0] + steps[1] * (na - 1), steps[2] * (na - 1) + steps[3])


def layout_of(tok, tokens):
    na = 4 if tok % 4 == 0 else tok
    nb = tok // na
    return na, nb, tokens // (4 * nb)


def plane(sizes):
    ngrp, nwid = sizes
    g, w = lax.axis_index("grp"), lax.axis_index("wid")
    spots = [
        ((d, e), lax.rem(g + d, ngrp), lax.rem(w + e, nwid))
        for d in range(ngrp) for e in range(nwid) if d or e
    ]
    return g * nwid + w, [(step, p * nwid + q, {"grp": p, "wid": q}) for step, p, q in spots]


def spreader(sizes, view, mine, sems):
    ngrp, nwid = sizes
    send, recv = sems
    g, w = lax.axis_index("grp"), lax.axis_index("wid")

    def copy(d, e, block, source=None):
        n = d * nwid + e - 1
        if e == 0:
            where = {"grp": lax.rem(g + d, ngrp)}
        else:
            where = {"wid": lax.rem(w + e, nwid)}
        here = view(block)
        return remote(here if source is None else source, here, send.at[n], recv.at[n], where)

    direct = [(d, 0) for d in range(1, ngrp)] + [(0, e) for e in range(1, nwid)]
    handed = [(d, e) for d in range(1, ngrp) for e in range(1, nwid)]

    def origin(d):
        return lax.rem(g + ngrp - d, ngrp) * nwid + w

    def first():
        for d, e in direct:
            copy(d, e, g * nwid + w, mine).start()

    def second():
        for d in range(1, ngrp):
            copy(d, 0, g * nwid + w).wait_recv()
        for d, e in handed:
            copy(d, e, origin(d)).start()

    def last():
        for e in range(1, nwid):
            copy(0, e, g * nwid + w).wait_recv()
        for d, e in handed:
            copy(d, e, origin(d)).wait_recv()

    def close():
        for d, e in direct + handed:
            copy(d, e, g * nwid + w).wait_send()

    return first, second, last, close


def forward_kernel(dims, counts, group, sizes, *refs):
    na, nb, jobs, slots = dims
    many = len(counts)
    x_ref = refs[0]
    weights = [refs[1 + 2 * i: 3 + 2 * i] for i in range(many)]
    downs = refs[1 + 2 * many: 1 + 3 * many]
    (
        x, out, kept, target, own, full, near,
        held, loaded, below, lowered, stored, total_of, shares, got,
        sx, rx, ss, rs, se, re, partial,
    ) = refs[1 + 3 * many: 23 + 3 * many]
    rest = refs[23 + 3 * many:]
    bufs, sems = rest[:8], rest[8:]
    starts = [sum(counts[:i]) for i in range(many + 1)]
    rows = out.shape[1]
    kept_jobs = kept.shape[2] // (2 * LANES * group)
    near_units = starts[many - 1]
    near_job = (near_units - 1) // group
    members, height, features = full.shape[1:]
    pieces = ss.shape[0]
    step = features // pieces
    me, places = plane(sizes)

    def fetch(ref, column, slot, u, i):
        return pltpu.make_async_copy(
            ref.at[:, pl.ds(pl.multiple_of(column, LANES), LANES)],
            held.at[slot, u, :, pl.ds(i * LANES, LANES)],
            loaded.at[slot, u, i],
        )

    def load(j):
        slot = lax.rem(j, SLOTS)
        for u in range(group):
            c = j * group + u
            for n, pair in enumerate(weights):
                @pl.when((c >= starts[n]) & (c < starts[n + 1]))
                def _(u=u, c=c, n=n, pair=pair):
                    for i in range(2):
                        fetch(pair[i], (c - starts[n]) * LANES, slot, u, i).start()

    def below_copy(c):
        slot = lax.rem(c, below.shape[0])
        row = pl.multiple_of((c - near_units) * LANES, LANES)
        return pltpu.make_async_copy(
            downs[many - 1].at[pl.ds(row, LANES), :], below.at[slot], lowered.at[slot]
        )

    def near_copy(n):
        height_n = counts[n] * LANES
        return pltpu.make_async_copy(
            downs[n], near.at[pl.ds(starts[n] * LANES, height_n), :], stored.at[n]
        )

    xs = spreader(sizes, lambda block: x.at[block], x_ref, (sx, rx))

    def share(n, p, k, block, where):
        cols = pl.ds(p * step, step)
        return remote(
            shares.at[n, block, :, cols], got.at[k, n, :, cols],
            ss.at[p, n, k], rs.at[p, n, k], where,
        )

    def give(n):
        for p in range(pieces):
            cols = pl.ds(p * step, step)
            shares[n, :, :, cols] = total_of[n, :, cols].astype(BF16).reshape(
                members, height, step
            )
            for k, (_, block, where) in enumerate(places):
                share(n, p, k, block, where).start()

    def prepare(barrier, count):
        for _, _, where in places:
            pl.semaphore_signal(barrier, inc=1, device_id=where, device_id_type=MESH)
        for j in range(min(SLOTS, jobs)):
            load(j)
        for n in range(many - 1):
            near_copy(n).start()
        for c in range(near_units, min(near_units + below.shape[0], starts[-1])):
            below_copy(c).start()
        total_of[...] = jnp.zeros_like(total_of)
        x[me] = x_ref[...]
        pl.semaphore_wait(barrier, count + len(places))
        xs[0]()
        xs[1]()
        xs[2]()

    def produce(j, part):
        slot = lax.rem(j, SLOTS)
        left = x[...].reshape(members * height, features)
        for u in range(group):
            for i in range(2):
                fetch(weights[0][0], 0, slot, u, i).wait()
            product = matmul(left, held[slot, u])
            partial[part, :, :, pl.ds(u * 2 * LANES, 2 * LANES)] = product.reshape(
                4 * nb, rows, 2 * LANES
            )

        @pl.when(j + SLOTS < jobs)
        def _():
            load(j + SLOTS)

    def finish(j, kind, block, total):
        for u in range(group):
            gate = total[:, u * 2 * LANES: u * 2 * LANES + LANES]
            up = total[:, u * 2 * LANES + LANES: (u + 1) * 2 * LANES]
            column = pl.multiple_of((j * group + u) * LANES, LANES)
            out[block, :, pl.ds(column, LANES)] = (
                gate / (1.0 + jnp.exp(-gate)) * up
            ).astype(BF16)

        @pl.when(j < kept_jobs)
        def _():
            wide = 2 * LANES * group
            kept[kind, :, pl.ds(pl.multiple_of(j * wide, LANES), wide)] = total

    def consume(j):
        for u in range(group):
            c = j * group + u
            column = pl.multiple_of(c * LANES, LANES)
            left = out[:, :, pl.ds(column, LANES)].reshape(members * height, LANES)
            for n in range(many - 1):
                @pl.when((c >= starts[n]) & (c < starts[n + 1]))
                def _(n=n, c=c, column=column, left=left):
                    pl.when(c == starts[n])(lambda: near_copy(n).wait())
                    total_of[n] += matmul(left, near[pl.ds(column, LANES), :])

            @pl.when(c >= near_units)
            def _(c=c, left=left):
                slot = lax.rem(c, below.shape[0])
                below_copy(c).wait()
                total_of[many - 1] += matmul(left, below[slot])

                @pl.when(c + below.shape[0] < starts[-1])
                def _():
                    below_copy(c + below.shape[0]).start()

        @pl.when(j == near_job)
        def _():
            for n in range(many - 1):
                give(n)

    close = relay(
        dims, FORWARD_STEPS, produce, finish, consume, partial, out, group * LANES, bufs,
        sems, prepare,
    )

    give(many - 1)
    spreads = []
    for p in range(pieces):
        cols = pl.ds(p * step, step)
        sums = []
        for n in range(many):
            total = shares[n, me, :, cols].astype(F32)
            for k, (_, block, where) in enumerate(places):
                share(n, p, k, block, where).wait_recv()
                total = total + got[k, n, :, cols].astype(F32)
            sums.append(total)
        goal = sums[-1].astype(BF16)
        target[:, cols] = goal
        goal = goal.astype(F32)
        for n in range(many - 1):
            value = (sums[n] - goal).astype(BF16)
            own[n, :, cols] = value
            full[n, me, :, cols] = value
        spread = spreader(
            sizes, lambda block, cols=cols: full.at[:, block, :, cols], own.at[:, :, cols],
            (se.at[p], re.at[p]),
        )
        spread[0]()
        spreads.append(spread)
    for spread in spreads:
        spread[1]()
    for spread in spreads:
        spread[2]()
    for spread in spreads + [xs]:
        spread[3]()
    for n in range(many):
        for p in range(pieces):
            for k, (_, block, where) in enumerate(places):
                share(n, p, k, block, where).wait_send()
    close()


def forward(inputs, weights, downs, tok, sizes):
    height, features = inputs.shape
    members = sizes[0] * sizes[1]
    tokens = members * height
    na, nb, rows = layout_of(tok, tokens)
    weights = [padded(w) for w in weights]
    downs = [jnp.pad(d, ((0, -d.shape[0] % LANES), (0, 0))) for d in downs]
    counts = [w.shape[1] // LANES for w in weights[::2]]
    many = len(counts)
    group = divisor(sum(counts), 3)
    jobs = sum(counts) // group
    dims = (na, nb, jobs, ring_slots(na, FORWARD_STEPS))
    kept_jobs = -(-(sum(counts[:-1]) + 1) // group)
    width = 2 * LANES * group
    pieces = max(features // 256, 1)
    vmem = pl.BlockSpec(memory_space=pltpu.VMEM)
    hbm = pl.BlockSpec(memory_space=pltpu.HBM)
    dma = pltpu.SemaphoreType.DMA
    shape = jax.ShapeDtypeStruct
    lower = 2 * group
    outs = pl.pallas_call(
        functools.partial(forward_kernel, dims, counts, group, sizes),
        out_shape=[
            shape((members, height, features), BF16),
            shape((4 * nb, rows, sum(counts) * LANES), BF16),
            shape((2, rows, kept_jobs * width), F32),
            shape((height, features), BF16),
            shape((many - 1, height, features), BF16),
            shape((many - 1, members, height, features), BF16),
        ],
        in_specs=[vmem] + [hbm] * (3 * many),
        out_specs=[vmem] * 6,
        scratch_shapes=[
            pltpu.VMEM((sum(counts[:-1]) * LANES, features), BF16),
            pltpu.VMEM((SLOTS, group, features, 2 * LANES), BF16), dma((SLOTS, group, 2)),
            pltpu.VMEM((lower, LANES, features), BF16), dma((lower,)), dma((many - 1,)),
            pltpu.VMEM((many, tokens, features), F32),
            pltpu.VMEM((many, members, height, features), BF16),
            pltpu.VMEM((members - 1, many, height, features), BF16),
            dma((members - 1,)), dma((members - 1,)),
            dma((pieces, many, members - 1)), dma((pieces, many, members - 1)),
            dma((pieces, members - 1)), dma((pieces, members - 1)),
        ] + relay_scratch(dims, rows, width),
        compiler_params=pltpu.CompilerParams(
            collective_id=2, has_side_effects=True, vmem_limit_bytes=FORWARD_MIB * MIB
        ),
        name="forward_exchange",
    )(inputs, *weights, *downs)
    return outs, counts, downs[:-1]


def backward_kernel(dims, counts, group, full, kept, *rest):
    na, nb, jobs, slots = dims
    many = len(counts)
    downs = rest[:many]
    out, near, stored, partial = rest[many: many + 4]
    bufs, sems = rest[many + 4: many + 12], rest[many + 12:]
    starts = [sum(counts[:i]) for i in range(many + 1)]
    rows = out.shape[1]
    features = full.shape[3]

    def near_copy(n, u, c):
        return pltpu.make_async_copy(
            downs[n].at[pl.ds(u * LANES, LANES), :],
            near.at[pl.ds(pl.multiple_of(c * LANES, LANES), LANES), :], stored.at[c],
        )

    def produce(j, part):
        for u in range(group):
            c = j * group + u
            for n in range(many):
                @pl.when((c >= starts[n]) & (c < starts[n + 1]))
                def _(u=u, c=c, n=n):
                    error = full[n].reshape(4 * nb * rows, features)
                    row = pl.multiple_of(c * LANES, LANES)
                    near_copy(n, 0, c).wait()
                    product = outer_cols(error, near[pl.ds(row, LANES), :])
                    partial[part, :, :, pl.ds(u * LANES, LANES)] = product.reshape(
                        4 * nb, rows, LANES
                    )

            @pl.when(c >= starts[many])
            def _(u=u):
                partial[part, :, :, pl.ds(u * LANES, LANES)] = jnp.zeros(
                    (4 * nb, rows, LANES), F32
                )

    def finish(j, kind, block, total):
        for u in range(group):
            column = pl.multiple_of((j * group + u) * 2 * LANES, LANES)
            gate = kept[kind, :, pl.ds(column, LANES)]
            up = kept[kind, :, pl.ds(column + LANES, LANES)]
            value = total[:, u * LANES: (u + 1) * LANES]
            s = 1.0 / (1.0 + jnp.exp(-gate))
            out[block, :, pl.ds(column, LANES)] = (
                value * up * s * (1.0 + gate * (1.0 - s))
            ).astype(BF16)
            out[block, :, pl.ds(column + LANES, LANES)] = (value * gate * s).astype(BF16)

    def prepare(barrier, count):
        for n in range(many):
            for u in range(counts[n]):
                near_copy(n, u, starts[n] + u).start()
        pl.semaphore_wait(barrier, count)

    relay(
        dims, BACKWARD_STEPS, produce, finish, lambda j: None, partial, out,
        group * 2 * LANES, bufs, sems, prepare,
    )()


def backward(full, downs, kept, counts, tok):
    tokens = full.shape[1] * full.shape[2]
    na, nb, rows = layout_of(tok, tokens)
    group = 2
    jobs = -(-sum(counts) // group)
    dims = (na, nb, jobs, ring_slots(na, BACKWARD_STEPS))
    vmem = pl.BlockSpec(memory_space=pltpu.VMEM)
    grads = pl.pallas_call(
        functools.partial(backward_kernel, dims, counts, group),
        out_shape=jax.ShapeDtypeStruct((4 * nb, rows, jobs * group * 2 * LANES), BF16),
        in_specs=[vmem] * 2 + [pl.BlockSpec(memory_space=pltpu.HBM)] * len(downs),
        out_specs=vmem,
        scratch_shapes=[
            pltpu.VMEM((sum(counts) * LANES, full.shape[3]), BF16),
            pltpu.SemaphoreType.DMA((sum(counts),)),
        ] + relay_scratch(dims, rows, group * LANES),
        compiler_params=pltpu.CompilerParams(
            collective_id=3, has_side_effects=True, vmem_limit_bytes=20 * MIB
        ),
        name="backward_exchange",
    )(full, kept, *downs)
    return grads.reshape(tokens, jobs * group * 2 * LANES)


def padded(x):
    return jnp.pad(x, ((0, 0), (0, -x.shape[1] % LANES)))


def outer_kernel(counts, columns, grads, hidden, full, target, own, *outs):
    many = len(counts)
    tokens = columns.shape[0]
    outs[0][...] = target[...]
    for n in range(many):
        outs[1 + n][...] = own[n]
    downs = outs[1 + many: 1 + 2 * many]
    sides = outs[1 + 2 * many:]
    left = columns[...].T
    c = 0
    for n, count in enumerate(counts):
        gate, up = sides[2 * n], sides[2 * n + 1]
        error = full[n].reshape(tokens, full.shape[3])
        height = downs[n].shape[0]
        at = c * LANES
        downs[n][...] = inner_rows(hidden[:, at: at + height], error).astype(BF16)
        for u in range(count):
            product = matmul(left, grads[:, c * 2 * LANES: (c + 1) * 2 * LANES]).astype(BF16)
            size = min(LANES, gate.shape[1] - u * LANES)
            gate[:, u * LANES: u * LANES + size] = product[:, :size]
            up[:, u * LANES: u * LANES + size] = product[:, LANES: LANES + size]
            c += 1


def weight_grads(columns, grads, hidden, full, target, own, counts, widths):
    tokens, features = columns.shape
    tile = LANES
    many, members, height = full.shape[:3]
    out_bytes = 6 * features * sum(widths)
    sides = [w for w in widths for _ in range(2)]
    shape = jax.ShapeDtypeStruct
    whole = pl.BlockSpec(memory_space=pltpu.VMEM)
    lane = pl.BlockSpec((height, tile), lambda i: (0, i))
    return pl.pallas_call(
        functools.partial(outer_kernel, counts),
        grid=(features // tile,),
        out_shape=[shape((height, features), BF16)] * (1 + many)
        + [shape((w, features), BF16) for w in widths]
        + [shape((features, w), BF16) for w in sides],
        in_specs=[
            pl.BlockSpec((tokens, tile), lambda i: (0, i)), whole, whole,
            pl.BlockSpec((many, members, height, tile), lambda i: (0, 0, 0, i)),
            lane, pl.BlockSpec((many, height, tile), lambda i: (0, 0, i)),
        ],
        out_specs=[lane] * (1 + many)
        + [pl.BlockSpec((w, tile), lambda i: (0, i)) for w in widths]
        + [pl.BlockSpec((tile, w), lambda i: (i, 0)) for w in sides],
        compiler_params=pltpu.CompilerParams(vmem_limit_bytes=24 * MIB),
        cost_estimate=pl.CostEstimate(
            flops=tokens * out_bytes, bytes_accessed=out_bytes, transcendentals=0
        ),
        name="weight_grads",
    )(columns, grads, hidden, full, target, own)


def body(
    tok, sizes, inputs, parent_gate, parent_up, parent_down, first_gate, first_up, first_down,
    second_gate, second_up, second_down,
):
    weights = (first_gate, first_up, second_gate, second_up, parent_gate, parent_up)
    downs = (first_down, second_down, parent_down)
    (x, hidden, kept, target, own, full), counts, nearest = forward(
        inputs, weights, downs, tok, sizes
    )
    tokens = x.shape[0] * x.shape[1]
    counts = counts[:-1]
    grads = backward(full, nearest, kept, counts, tok)
    near_hidden = hidden.reshape(tokens, -1)
    (
        target, first_error, second_error, first_grad_down, second_grad_down,
        first_grad_gate, first_grad_up, second_grad_gate, second_grad_up,
    ) = weight_grads(
        x.reshape(tokens, -1), grads, near_hidden, full, target, own, counts,
        [first_gate.shape[1], second_gate.shape[1]],
    )
    return (
        target, first_error, second_error,
        first_grad_gate, first_grad_up, first_grad_down,
        second_grad_gate, second_grad_up, second_grad_down,
    )


def solution(mesh):
    tok = mesh.shape["tok"]
    sizes = (mesh.shape["grp"], mesh.shape["wid"])
    rows = P(("grp", "wid"), "tok")
    cols = P("tok", ("grp", "wid"))
    return jax.shard_map(
        functools.partial(body, tok, sizes),
        mesh=mesh,
        in_specs=(rows, cols, cols, rows, cols, cols, rows, cols, cols, rows),
        out_specs=(rows, rows, rows, cols, cols, rows, cols, cols, rows),
        check_vma=False,
    )
```

time: 197 us -> 172 us (0.87)
  matrix products: 13.8 us -> 0 us
  Pallas kernels: 179 us -> 170 us
  local copies, waits for them, and re-layouts: 3.47 us -> 0.99 us
    dot_general x10 -> x0, matrix products: 13.8 us -> none  [the longest x6 5.9 us: matmul(): return jnp.dot(left, right, preferred_element_type=F32)]
    pallas_call x5 -> x3, Pallas kernels: 179 us -> 170 us  [the longest x1 116 us: forward(): pl.pallas_call(functools.partial(forward_kernel, dims, counts, group, siz...]
    unnamed x23 -> x6, local copies, waits for them, and re-layouts: 3.47 us -> 0.99 us
where the time goes in v1:
time: 172 us; the launch traced here: 171 us
  Pallas kernels  170 us (99%)
    pallas_call x1, Pallas kernels, forward(): pl.pallas_call(functools.partial(forward_kernel, dims, counts, group, siz...  116 us
    pallas_call x1, Pallas kernels, backward(): pl.pallas_call(functools.partial(backward_kernel, dims, counts, group), o...  45.2 us
    pallas_call x1, Pallas kernels, weight_grads(): pl.pallas_call(functools.partial(outer_kernel, counts), grid=(features //...  8.86 us

profile of v1, /device:TPU:0, one launch (start us, length us, event | category | flops | bytes accessed | tf_op | source)
XLA Modules:
  0.0 171.4 jit_solution(2438802880857037829)
XLA Ops:
  0.6 0.0 copy-start.1
  0.7 0.0 copy-start
  0.7 0.0 copy-start.2
  0.7 1.0 copy-done.2
  1.7 115.7 %forward_exchange.1 = (bf16[4,32,1024]{2,1,0:T(8,128)(2,1)S(1)}, bf16[8,16,10368]{2,1,0:T(8,128)(2,1)S(1)}, f32[2,16,6912]{2,1,0:T(8,128)S(1)}, bf16[32,1024]{1,...) custom-call(bf16[32,1024]{1,0:T(8,128)(2,1)S(1)} %copy-done.2, ...), custom_call_target="tpu_custom_call" | custom-call | tf_op jit(solution)/shard_map/forward_exchange/pallas_call | solution.py:565
  117.3 0.0 copy-done.1
  117.3 0.0 copy-done
  117.3 45.2 %backward_exchange.1 = bf16[8,16,6656]{2,1,0:T(8,128)(2,1)S(1)} custom-call(bf16[2,4,32,1024]{3,2,1,0:T(8,128)(2,1)S(1)} %get-tuple-element.25.full, f32[2,16,6912]{2,1,0:T(8,128)S(1)} %get-tuple-element.26.kept, bf16[1792,1024]{1,0:T(8,128)(2,1)S(1)} %copy-done, bf16[1408,1024]{1,0:T(8,128)(2,1)S(1)} %copy-done.1), custom_call_target="tpu_custom_call" | custom-call | tf_op jit(solution)/shard_map/backward_exchange/pallas_call | solution.py:663
  162.5 8.9 %weight_grads.1 = (bf16[32,1024]{1,0:T(8,128)(2,1)}, bf16[32,1024]{1,0:T(8,128)(2,1)}, bf16[32,1024]{1,0:T(8,128)(2,1)}, bf16[1792,1024]{1,0:T(8,128)(2,1)}, bf1...) custom-call(bf16[128,1024]{1,0:T(8,128)(2,1)S(1)} %bitcast.5, ...), custom_call_target="tpu_custom_call" | custom-call | flops 2516582400 | bytes 19660800 | tf_op jit(solution)/shard_map/weight_grads/pallas_call | solution.py:717
Async XLA Ops:
  0.6 116.7 %copy-start.1 = (bf16[1408,1024]{1,0:T(8,128)(2,1)S(1)}, bf16[1408,1024]{1,0:T(8,128)(2,1)}, u32[]{:S(2)}) copy-start(bf16[1408,1024]{1,0:T(8,128)(2,1)} %rest_1_.1) | copy-start | bytes 8650756
  0.7 116.7 %copy-start = (bf16[1792,1024]{1,0:T(8,128)(2,1)S(1)}, bf16[1792,1024]{1,0:T(8,128)(2,1)}, u32[]{:S(2)}) copy-start(bf16[1792,1024]{1,0:T(8,128)(2,1)} %rest_0_.1) | copy-start | bytes 11010052
  0.7 1.0 copy-start.2

commit v2 on v1

--- a/solution.py
+++ b/solution.py
@@ -11,19 +11,17 @@
 LANES = 128
 MIB = 1024 * 1024
 SLOTS = 4
-FORWARD_STEPS = (2, 2, 2, 1, 2, 2, 2)
-BACKWARD_STEPS = (3, 3, 3, 3, 4, 3, 2)
-FORWARD_MIB = 48
+FORWARD_STEPS = (2, 2, 2, 2, 2, 2, 2)
+BACKWARD_STEPS = (2, 2, 2, 2, 2, 2, 2)
+FORWARD_GROUP = 3
+BACKWARD_GROUP = 4
+STEP_MIB = 50
 F32 = jnp.float32
 BF16 = jnp.bfloat16
 
 
 def matmul(left, right):
     return jnp.dot(left, right, preferred_element_type=F32)
-
-
-def inner_rows(left, right):
-    return lax.dot_general(left, right, (((0,), (0,)), ((), ())), preferred_element_type=F32)
 
 
 def outer_cols(left, right):
@@ -35,10 +33,6 @@
         src_ref=src, dst_ref=dst, send_sem=send, recv_sem=recv,
         device_id=where, device_id_type=MESH,
     )
-
-
-def divisor(total, most):
-    return max(k for k in range(1, most + 1) if total % k == 0)
 
 
 def relay(dims, steps, produce, finish, consume, partial, out, span, bufs, sems, prepare):
@@ -61,14 +55,15 @@
     end = (hi == 0) | (hi == na - 1)
     turn = jnp.where(hi == na - 1, 0, 1)
 
-    barrier = pltpu.get_barrier_semaphore()
-    for where in beside:
-        pl.semaphore_signal(barrier, inc=1, device_id=where, device_id_type=MESH)
-    for d in range(2):
-        @pl.when(pos[d] < na - 1)
-        def _(d=d):
-            pl.semaphore_signal(barrier, inc=1, device_id=onward[d], device_id_type=MESH)
-    prepare(barrier, side + jnp.where(end, 1, 2))
+    if prepare is not None:
+        barrier = pltpu.get_barrier_semaphore()
+        for where in beside:
+            pl.semaphore_signal(barrier, inc=1, device_id=where, device_id_type=MESH)
+        for d in range(2):
+            @pl.when(pos[d] < na - 1)
+            def _(d=d):
+                pl.semaphore_signal(barrier, inc=1, device_id=onward[d], device_id_type=MESH)
+        prepare(barrier, side + jnp.where(end, 1, 2))
 
     def a_block(y, d):
         return y * 2 + d
@@ -111,16 +106,22 @@
         inside = (j >= 0) & (j < jobs)
         return pl.when(inside if condition is None else inside & condition)
 
-    def begin(j):
+    def ready(j):
         slot = lax.rem(j, slots)
         produce(j, slot)
         for k in range(side):
             ay_out[j, k] = partial[slot, pl.ds(peers[k] * 2, 2)].astype(BF16)
-            copy_ay(j, k).start()
         for d in range(2):
             @pl.when(pos[d] == 0)
             def _(d=d):
                 bz_out[j, d] = partial[slot, pl.ds(b_block(0, d), nb)].astype(BF16)
+
+    def begin(j):
+        for k in range(side):
+            copy_ay(j, k).start()
+        for d in range(2):
+            @pl.when(pos[d] == 0)
+            def _(d=d):
                 copy_bz(j, d).start()
 
     def pair(j):
@@ -238,6 +239,7 @@
         for d in range(2):
             j = t - leave_at - open_b * far[d]
             on(j, far[d] > 0)(functools.partial(pass_b, j, d))
+        on(t + 1)(functools.partial(ready, t + 1))
         j = t - done
         on(j)(functools.partial(arrive, j))
         return carry
@@ -248,6 +250,7 @@
                 spread_ay(j, d, k).wait_recv()
         consume(j)
 
+    ready(0)
     lax.fori_loop(0, jobs + done, tick, 0)
 
     def drain(j, carry):
@@ -296,7 +299,7 @@
 
 
 def ring_slots(na, steps):
-    return 1 + max(steps[0] + steps[1] * (na - 1), steps[2] * (na - 1) + steps[3])
+    return 2 + max(steps[0] + steps[1] * (na - 1), steps[2] * (na - 1) + steps[3])
 
 
 def layout_of(tok, tokens):
@@ -358,19 +361,20 @@
     return first, second, last, close
 
 
-def forward_kernel(dims, counts, group, sizes, *refs):
+def step_kernel(dims, dims_back, counts, group, sizes, *refs):
     na, nb, jobs, slots = dims
     many = len(counts)
     x_ref = refs[0]
     weights = [refs[1 + 2 * i: 3 + 2 * i] for i in range(many)]
     downs = refs[1 + 2 * many: 1 + 3 * many]
     (
-        x, out, kept, target, own, full, near,
+        x, turned, target, own, full, grads, out, kept, near,
         held, loaded, below, lowered, stored, total_of, shares, got,
-        sx, rx, ss, rs, se, re, partial,
-    ) = refs[1 + 3 * many: 23 + 3 * many]
-    rest = refs[23 + 3 * many:]
-    bufs, sems = rest[:8], rest[8:]
+        sx, rx, ss, rs, se, re,
+    ) = refs[1 + 3 * many: 24 + 3 * many]
+    rest = refs[24 + 3 * many:]
+    partial, bufs, sems = rest[0], rest[1:9], rest[9:25]
+    partial_back, bufs_back, sems_back = rest[25], rest[26:34], rest[34:]
     starts = [sum(counts[:i]) for i in range(many + 1)]
     rows = out.shape[1]
     kept_jobs = kept.shape[2] // (2 * LANES * group)
@@ -449,12 +453,23 @@
         slot = lax.rem(j, SLOTS)
         left = x[...].reshape(members * height, features)
         for u in range(group):
-            for i in range(2):
-                fetch(weights[0][0], 0, slot, u, i).wait()
-            product = matmul(left, held[slot, u])
-            partial[part, :, :, pl.ds(u * 2 * LANES, 2 * LANES)] = product.reshape(
-                4 * nb, rows, 2 * LANES
-            )
+            c = j * group + u
+
+            @pl.when(c < starts[-1])
+            def _(u=u):
+                for i in range(2):
+                    fetch(weights[0][0], 0, slot, u, i).wait()
+                product = matmul(left, held[slot, u])
+                partial[part, :, :, pl.ds(u * 2 * LANES, 2 * LANES)] = product.reshape(
+                    4 * nb, rows, 2 * LANES
+                )
+
+            if starts[-1] % group:
+                @pl.when(c >= starts[-1])
+                def _(u=u):
+                    partial[part, :, :, pl.ds(u * 2 * LANES, 2 * LANES)] = jnp.zeros(
+                        (4 * nb, rows, 2 * LANES), F32
+                    )
 
         @pl.when(j + SLOTS < jobs)
         def _():
@@ -479,13 +494,18 @@
             c = j * group + u
             column = pl.multiple_of(c * LANES, LANES)
             left = out[:, :, pl.ds(column, LANES)].reshape(members * height, LANES)
+
+            @pl.when(c < near_units)
+            def _(column=column, left=left):
+                turned[pl.ds(column, LANES), :] = left.T
+
             for n in range(many - 1):
                 @pl.when((c >= starts[n]) & (c < starts[n + 1]))
                 def _(n=n, c=c, column=column, left=left):
                     pl.when(c == starts[n])(lambda: near_copy(n).wait())
                     total_of[n] += matmul(left, near[pl.ds(column, LANES), :])
 
-            @pl.when(c >= near_units)
+            @pl.when((c >= near_units) & (c < starts[-1]))
             def _(c=c, left=left):
                 slot = lax.rem(c, below.shape[0])
                 below_copy(c).wait()
@@ -533,6 +553,9 @@
         spread[1]()
     for spread in spreads:
         spread[2]()
+    close_back = backward_relay(
+        dims_back, counts[:-1], full, near, kept, grads, partial_back, bufs_back, sems_back
+    )
     for spread in spreads + [xs]:
         spread[3]()
     for n in range(many):
@@ -540,6 +563,7 @@
             for k, (_, block, where) in enumerate(places):
                 share(n, p, k, block, where).wait_send()
     close()
+    close_back()
 
 
 def forward(inputs, weights, downs, tok, sizes):
@@ -551,10 +575,10 @@
     downs = [jnp.pad(d, ((0, -d.shape[0] % LANES), (0, 0))) for d in downs]
     counts = [w.shape[1] // LANES for w in weights[::2]]
     many = len(counts)
-    group = divisor(sum(counts), 3)
-    jobs = sum(counts) // group
-    dims = (na, nb, jobs, ring_slots(na, FORWARD_STEPS))
-    kept_jobs = -(-(sum(counts[:-1]) + 1) // group)
+    group = FORWARD_GROUP
+    jobs = -(-sum(counts) // group)
+    dims = (na, nb, jobs, min(jobs, ring_slots(na, FORWARD_STEPS)))
+    kept_jobs = -(-(sum(counts[:-1]) + BACKWARD_GROUP - 1) // group)
     width = 2 * LANES * group
     pieces = max(features // 256, 1)
     vmem = pl.BlockSpec(memory_space=pltpu.VMEM)
@@ -562,20 +586,25 @@
     dma = pltpu.SemaphoreType.DMA
     shape = jax.ShapeDtypeStruct
     lower = 2 * group
+    near_units = sum(counts[:-1])
+    jobs_back = -(-near_units // BACKWARD_GROUP)
+    dims_back = (na, nb, jobs_back, min(jobs_back, ring_slots(na, BACKWARD_STEPS)))
     outs = pl.pallas_call(
-        functools.partial(forward_kernel, dims, counts, group, sizes),
+        functools.partial(step_kernel, dims, dims_back, counts, group, sizes),
         out_shape=[
             shape((members, height, features), BF16),
-            shape((4 * nb, rows, sum(counts) * LANES), BF16),
-            shape((2, rows, kept_jobs * width), F32),
+            shape((near_units * LANES, tokens), BF16),
             shape((height, features), BF16),
             shape((many - 1, height, features), BF16),
             shape((many - 1, members, height, features), BF16),
+            shape((4 * nb, rows, jobs_back * BACKWARD_GROUP * 2 * LANES), BF16),
         ],
         in_specs=[vmem] + [hbm] * (3 * many),
         out_specs=[vmem] * 6,
         scratch_shapes=[
-            pltpu.VMEM((sum(counts[:-1]) * LANES, features), BF16),
+            pltpu.VMEM((4 * nb, rows, jobs * group * LANES), BF16),
+            pltpu.VMEM((2, rows, kept_jobs * width), F32),
+            pltpu.VMEM((near_units * LANES, features), BF16),
             pltpu.VMEM((SLOTS, group, features, 2 * LANES), BF16), dma((SLOTS, group, 2)),
             pltpu.VMEM((lower, LANES, features), BF16), dma((lower,)), dma((many - 1,)),
             pltpu.VMEM((many, tokens, features), F32),
@@ -584,30 +613,23 @@
             dma((members - 1,)), dma((members - 1,)),
             dma((pieces, many, members - 1)), dma((pieces, many, members - 1)),
             dma((pieces, members - 1)), dma((pieces, members - 1)),
-        ] + relay_scratch(dims, rows, width),
+        ] + relay_scratch(dims, rows, width)
+        + relay_scratch(dims_back, rows, BACKWARD_GROUP * LANES),
         compiler_params=pltpu.CompilerParams(
-            collective_id=2, has_side_effects=True, vmem_limit_bytes=FORWARD_MIB * MIB
+            collective_id=2, has_side_effects=True, vmem_limit_bytes=STEP_MIB * MIB
         ),
-        name="forward_exchange",
+        name="distill_step",
     )(inputs, *weights, *downs)
-    return outs, counts, downs[:-1]
-
-
-def backward_kernel(dims, counts, group, full, kept, *rest):
+    return outs, counts
+
+
+def backward_relay(dims, counts, full, near, kept, out, partial, bufs, sems):
     na, nb, jobs, slots = dims
     many = len(counts)
-    downs = rest[:many]
-    out, near, stored, partial = rest[many: many + 4]
-    bufs, sems = rest[many + 4: many + 12], rest[many + 12:]
+    group = BACKWARD_GROUP
     starts = [sum(counts[:i]) for i in range(many + 1)]
     rows = out.shape[1]
     features = full.shape[3]
-
-    def near_copy(n, u, c):
-        return pltpu.make_async_copy(
-            downs[n].at[pl.ds(u * LANES, LANES), :],
-            near.at[pl.ds(pl.multiple_of(c * LANES, LANES), LANES), :], stored.at[c],
-        )
 
     def produce(j, part):
         for u in range(group):
@@ -617,7 +639,6 @@
                 def _(u=u, c=c, n=n):
                     error = full[n].reshape(4 * nb * rows, features)
                     row = pl.multiple_of(c * LANES, LANES)
-                    near_copy(n, 0, c).wait()
                     product = outer_cols(error, near[pl.ds(row, LANES), :])
                     partial[part, :, :, pl.ds(u * LANES, LANES)] = product.reshape(
                         4 * nb, rows, LANES
@@ -641,47 +662,17 @@
             ).astype(BF16)
             out[block, :, pl.ds(column + LANES, LANES)] = (value * gate * s).astype(BF16)
 
-    def prepare(barrier, count):
-        for n in range(many):
-            for u in range(counts[n]):
-                near_copy(n, u, starts[n] + u).start()
-        pl.semaphore_wait(barrier, count)
-
-    relay(
+    return relay(
         dims, BACKWARD_STEPS, produce, finish, lambda j: None, partial, out,
-        group * 2 * LANES, bufs, sems, prepare,
-    )()
-
-
-def backward(full, downs, kept, counts, tok):
-    tokens = full.shape[1] * full.shape[2]
-    na, nb, rows = layout_of(tok, tokens)
-    group = 2
-    jobs = -(-sum(counts) // group)
-    dims = (na, nb, jobs, ring_slots(na, BACKWARD_STEPS))
-    vmem = pl.BlockSpec(memory_space=pltpu.VMEM)
-    grads = pl.pallas_call(
-        functools.partial(backward_kernel, dims, counts, group),
-        out_shape=jax.ShapeDtypeStruct((4 * nb, rows, jobs * group * 2 * LANES), BF16),
-        in_specs=[vmem] * 2 + [pl.BlockSpec(memory_space=pltpu.HBM)] * len(downs),
-        out_specs=vmem,
-        scratch_shapes=[
-            pltpu.VMEM((sum(counts) * LANES, full.shape[3]), BF16),
-            pltpu.SemaphoreType.DMA((sum(counts),)),
-        ] + relay_scratch(dims, rows, group * LANES),
-        compiler_params=pltpu.CompilerParams(
-            collective_id=3, has_side_effects=True, vmem_limit_bytes=20 * MIB
-        ),
-        name="backward_exchange",
-    )(full, kept, *downs)
-    return grads.reshape(tokens, jobs * group * 2 * LANES)
+        group * 2 * LANES, bufs, sems, None,
+    )
 
 
 def padded(x):
     return jnp.pad(x, ((0, 0), (0, -x.shape[1] % LANES)))
 
 
-def outer_kernel(counts, columns, grads, hidden, full, target, own, *outs):
+def outer_kernel(counts, columns, grads, turned, full, target, own, *outs):
     many = len(counts)
     tokens = columns.shape[0]
     outs[0][...] = target[...]
@@ -696,7 +687,7 @@
         error = full[n].reshape(tokens, full.shape[3])
         height = downs[n].shape[0]
         at = c * LANES
-        downs[n][...] = inner_rows(hidden[:, at: at + height], error).astype(BF16)
+        downs[n][...] = matmul(turned[at: at + height, :], error).astype(BF16)
         for u in range(count):
             product = matmul(left, grads[:, c * 2 * LANES: (c + 1) * 2 * LANES]).astype(BF16)
             size = min(LANES, gate.shape[1] - u * LANES)
@@ -705,9 +696,9 @@
             c += 1
 
 
-def weight_grads(columns, grads, hidden, full, target, own, counts, widths):
+def weight_grads(columns, grads, turned, full, target, own, counts, widths):
     tokens, features = columns.shape
-    tile = LANES
+    tile = 2 * LANES if features % (2 * LANES) == 0 else features
     many, members, height = full.shape[:3]
     out_bytes = 6 * features * sum(widths)
     sides = [w for w in widths for _ in range(2)]
@@ -728,12 +719,12 @@
         out_specs=[lane] * (1 + many)
         + [pl.BlockSpec((w, tile), lambda i: (0, i)) for w in widths]
         + [pl.BlockSpec((tile, w), lambda i: (i, 0)) for w in sides],
-        compiler_params=pltpu.CompilerParams(vmem_limit_bytes=24 * MIB),
+        compiler_params=pltpu.CompilerParams(vmem_limit_bytes=40 * MIB),
         cost_estimate=pl.CostEstimate(
             flops=tokens * out_bytes, bytes_accessed=out_bytes, transcendentals=0
         ),
         name="weight_grads",
-    )(columns, grads, hidden, full, target, own)
+    )(columns, grads, turned, full, target, own)
 
 
 def body(
@@ -742,18 +733,16 @@
 ):
     weights = (first_gate, first_up, second_gate, second_up, parent_gate, parent_up)
     downs = (first_down, second_down, parent_down)
-    (x, hidden, kept, target, own, full), counts, nearest = forward(
+    (x, turned, target, own, full, grads), counts = forward(
         inputs, weights, downs, tok, sizes
     )
     tokens = x.shape[0] * x.shape[1]
     counts = counts[:-1]
-    grads = backward(full, nearest, kept, counts, tok)
-    near_hidden = hidden.reshape(tokens, -1)
     (
         target, first_error, second_error, first_grad_down, second_grad_down,
         first_grad_gate, first_grad_up, second_grad_gate, second_grad_up,
     ) = weight_grads(
-        x.reshape(tokens, -1), grads, near_hidden, full, target, own, counts,
+        x.reshape(tokens, -1), grads.reshape(tokens, -1), turned, full, target, own, counts,
         [first_gate.shape[1], second_gate.shape[1]],
     )
     return (

time: 172 us -> 158 us (0.919)
  Pallas kernels: 170 us -> 157 us
    pallas_call x2 -> x1, Pallas kernels: 161 us -> 148 us  [forward(): pl.pallas_call(functools.partial(step_kernel, dims, dims_back, counts, gr...]
where the time goes in v2:
time: 158 us
  Pallas kernels  157 us (99%)
    pallas_call x1, Pallas kernels, forward(): pl.pallas_call(functools.partial(step_kernel, dims, dims_back, counts, gr...  148 us
    pallas_call x1, Pallas kernels, weight_grads(): pl.pallas_call(functools.partial(outer_kernel, counts), grid=(features //...  8.82 us

profile of v2, /device:TPU:0, one launch (start us, length us, event | category | flops | bytes accessed | tf_op | source)
XLA Modules:
  0.0 158.1 jit_solution(15974162226446816424)
XLA Ops:
  0.6 0.0 copy-start
  0.7 0.8 copy-done
  1.5 147.8 %distill_step.1 = (bf16[4,32,1024]{2,1,0:T(8,128)(2,1)S(1)}, bf16[3200,128]{1,0:T(8,128)(2,1)S(1)}, bf16[32,1024]{1,0:T(8,128)(2,1)S(1)}, bf16[2,32,1024]{2,1,0:...) custom-call(bf16[32,1024]{1,0:T(8,128)(2,1)S(1)} %copy-done, ...), custom_call_target="tpu_custom_call" | custom-call | tf_op jit(solution)/shard_map/distill_step/pallas_call | solution.py:592
  149.3 8.8 %weight_grads.1 = (bf16[32,1024]{1,0:T(8,128)(2,1)}, bf16[32,1024]{1,0:T(8,128)(2,1)}, bf16[32,1024]{1,0:T(8,128)(2,1)}, bf16[1792,1024]{1,0:T(8,128)(2,1)}, bf1...) custom-call(bf16[128,1024]{1,0:T(8,128)(2,1)S(1)} %bitcast.3, ...), custom_call_target="tpu_custom_call" | custom-call | flops 2516582400 | bytes 19660800 | tf_op jit(solution)/shard_map/weight_grads/pallas_call | solution.py:708
Async XLA Ops:
  0.6 0.8 copy-start

commit v3 on v2

--- a/solution.py
+++ b/solution.py
@@ -11,10 +11,10 @@
 LANES = 128
 MIB = 1024 * 1024
 SLOTS = 4
-FORWARD_STEPS = (2, 2, 2, 2, 2, 2, 2)
+FORWARD_STEPS = (3, 3, 3, 3, 3, 3, 3)
 BACKWARD_STEPS = (2, 2, 2, 2, 2, 2, 2)
 FORWARD_GROUP = 3
-BACKWARD_GROUP = 4
+BACKWARD_GROUP = 5
 STEP_MIB = 50
 F32 = jnp.float32
 BF16 = jnp.bfloat16
@@ -75,32 +75,32 @@
         return out.at[pl.ds(block, count), :, pl.ds(pl.multiple_of(j * span, LANES), span)]
 
     def copy_ay(j, k):
-        return remote(ay_out.at[j, k], ay_in.at[j, k], say.at[j, k], ray.at[j, k], beside[k])
+        return remote(ay_out.at[j, k], ay_in.at[j, k], say.at[k], ray.at[j, k], beside[k])
 
     def copy_az(j, d):
-        return remote(az_out.at[j, d], az_in.at[j, d], saz.at[j, d], raz.at[j, d], onward[d])
+        return remote(az_out.at[j, d], az_in.at[j, d], saz.at[d], raz.at[j, d], onward[d])
 
     def copy_bz(j, d):
-        return remote(bz_out.at[j, d], bz_in.at[j, d], sbz.at[j, d], rbz.at[j, d], onward[d])
+        return remote(bz_out.at[j, d], bz_in.at[j, d], sbz.at[d], rbz.at[j, d], onward[d])
 
     def copy_by(j, k):
-        return remote(by_out.at[j, k], by_in.at[j, k], sby.at[j, k], rby.at[j, k], beside[k])
+        return remote(by_out.at[j, k], by_in.at[j, k], sby.at[k], rby.at[j, k], beside[k])
 
     def spread_az(j, d):
         here = piece(a_block(lo, d), j)
-        return remote(here, here, taz.at[j, d], uaz.at[j, d], back[d])
+        return remote(here, here, taz.at[d], uaz.at[j, d], back[d])
 
     def spread_ay(j, d, k):
         here = piece(a_block(lo, d), j)
-        return remote(here, here, tay.at[j, d, k], uay.at[j, d, k], beside[k])
+        return remote(here, here, tay.at[d, k], uay.at[j, d, k], beside[k])
 
     def spread_by(j, k):
         here = piece(b_block(lo, turn), j)
-        return remote(here, here, tby.at[j, k], uby.at[j, k], beside[k])
+        return remote(here, here, tby.at[k], uby.at[j, k], beside[k])
 
     def spread_bz(j, d):
         here = piece(b_block(0, d), j, nb)
-        return remote(here, here, tbz.at[j, d], ubz.at[j, d], back[d])
+        return remote(here, here, tbz.at[d], ubz.at[j, d], back[d])
 
     def on(j, condition=None):
         inside = (j >= 0) & (j < jobs)
@@ -253,31 +253,41 @@
     ready(0)
     lax.fori_loop(0, jobs + done, tick, 0)
 
-    def drain(j, carry):
-        for k in range(side):
-            copy_ay(j, k).wait_send()
+    def drain():
+        def spent(block, count, send, recv, where):
+            here = out.at[pl.ds(block, count)]
+            remote(here, here, send, recv, where).wait_send()
+
+        for k in range(side):
+            remote(
+                ay_out.at[:, k], ay_in.at[:, k], say.at[k], ray.at[0, k], beside[k]
+            ).wait_send()
             for d in range(2):
-                spread_ay(j, d, k).wait_send()
+                spent(a_block(lo, d), 1, tay.at[d, k], uay.at[0, d, k], beside[k])
         for d in range(2):
             @pl.when(pos[d] < na - 1)
             def _(d=d):
-                copy_az(j, d).wait_send()
-                copy_bz(j, d).wait_send()
+                remote(
+                    az_out.at[:, d], az_in.at[:, d], saz.at[d], raz.at[0, d], onward[d]
+                ).wait_send()
+                remote(
+                    bz_out.at[:, d], bz_in.at[:, d], sbz.at[d], rbz.at[0, d], onward[d]
+                ).wait_send()
 
             @pl.when(far[d] < na - 1)
             def _(d=d):
-                spread_az(j, d).wait_send()
-                spread_bz(j, d).wait_send()
+                spent(a_block(lo, d), 1, taz.at[d], uaz.at[0, d], back[d])
+                spent(b_block(0, d), nb, tbz.at[d], ubz.at[0, d], back[d])
 
         @pl.when(end)
         def _():
             for k in range(side):
-                copy_by(j, k).wait_send()
-                spread_by(j, k).wait_send()
-
-        return carry
-
-    return lambda: lax.fori_loop(0, jobs, drain, 0)
+                remote(
+                    by_out.at[:, k], by_in.at[:, k], sby.at[k], rby.at[0, k], beside[k]
+                ).wait_send()
+                spent(b_block(lo, turn), 1, tby.at[k], uby.at[0, k], beside[k])
+
+    return drain
 
 
 def relay_scratch(dims, rows, width):
@@ -293,7 +303,7 @@
         room(2, nb), room(2, nb), room(side), room(side),
     ]
     counts = [(side,), (2,), (2,), (side,), (2, side), (2,), (2,), (side,)]
-    sems = [dma((jobs,) + c) for c in counts for _ in range(2)]
+    sems = [dma(lead + c) for c in counts for lead in ((), (jobs,))]
     partial = pltpu.VMEM((slots, 4 * nb, rows, width), F32)
     return [partial] + bufs + sems
 
@@ -381,33 +391,48 @@
     near_units = starts[many - 1]
     near_job = (near_units - 1) // group
     members, height, features = full.shape[1:]
-    pieces = ss.shape[0]
+    pieces = rs.shape[0]
     step = features // pieces
     me, places = plane(sizes)
 
-    def fetch(ref, column, slot, u, i):
-        return pltpu.make_async_copy(
-            ref.at[:, pl.ds(pl.multiple_of(column, LANES), LANES)],
-            held.at[slot, u, :, pl.ds(i * LANES, LANES)],
-            loaded.at[slot, u, i],
-        )
+    cases = cases_of(starts, group, jobs)
+    first_below = near_units // group
+    depth = below.shape[0]
+    side_width = group * LANES
+
+    def between(j, low, high):
+        return pl.when((j >= low) & (j < high))
+
+    def window(at, size):
+        return pl.ds(pl.multiple_of(at * LANES, LANES), size * LANES)
 
     def load(j):
         slot = lax.rem(j, SLOTS)
-        for u in range(group):
-            c = j * group + u
-            for n, pair in enumerate(weights):
-                @pl.when((c >= starts[n]) & (c < starts[n + 1]))
-                def _(u=u, c=c, n=n, pair=pair):
+        for low, high, spans in cases:
+            @between(j, low, high)
+            def _(spans=spans):
+                for n, u, v in spans:
                     for i in range(2):
-                        fetch(pair[i], (c - starts[n]) * LANES, slot, u, i).start()
-
-    def below_copy(c):
-        slot = lax.rem(c, below.shape[0])
-        row = pl.multiple_of((c - near_units) * LANES, LANES)
+                        pltpu.make_async_copy(
+                            weights[n][i].at[:, window(j * group + u - starts[n], v - u)],
+                            held.at[slot, :, pl.ds(i * side_width + u * LANES, (v - u) * LANES)],
+                            loaded.at[slot],
+                        ).start()
+
+    def below_copy(j, u, v):
+        slot = lax.rem(j, depth)
         return pltpu.make_async_copy(
-            downs[many - 1].at[pl.ds(row, LANES), :], below.at[slot], lowered.at[slot]
+            downs[many - 1].at[window(j * group + u - near_units, v - u), :],
+            below.at[slot, pl.ds(u * LANES, (v - u) * LANES), :], lowered.at[slot],
         )
+
+    def load_below(j):
+        for low, high, spans in cases:
+            for n, u, v in spans:
+                if n == many - 1:
+                    @between(j, low, high)
+                    def _(u=u, v=v):
+                        below_copy(j, u, v).start()
 
     def near_copy(n):
         height_n = counts[n] * LANES
@@ -421,7 +446,7 @@
         cols = pl.ds(p * step, step)
         return remote(
             shares.at[n, block, :, cols], got.at[k, n, :, cols],
-            ss.at[p, n, k], rs.at[p, n, k], where,
+            ss.at[n, k], rs.at[p, n, k], where,
         )
 
     def give(n):
@@ -440,8 +465,8 @@
             load(j)
         for n in range(many - 1):
             near_copy(n).start()
-        for c in range(near_units, min(near_units + below.shape[0], starts[-1])):
-            below_copy(c).start()
+        for j in range(first_below, min(first_below + depth, jobs)):
+            load_below(j)
         total_of[...] = jnp.zeros_like(total_of)
         x[me] = x_ref[...]
         pl.semaphore_wait(barrier, count + len(places))
@@ -452,37 +477,18 @@
     def produce(j, part):
         slot = lax.rem(j, SLOTS)
         left = x[...].reshape(members * height, features)
-        for u in range(group):
-            c = j * group + u
-
-            @pl.when(c < starts[-1])
-            def _(u=u):
-                for i in range(2):
-                    fetch(weights[0][0], 0, slot, u, i).wait()
-                product = matmul(left, held[slot, u])
-                partial[part, :, :, pl.ds(u * 2 * LANES, 2 * LANES)] = product.reshape(
-                    4 * nb, rows, 2 * LANES
-                )
-
-            if starts[-1] % group:
-                @pl.when(c >= starts[-1])
-                def _(u=u):
-                    partial[part, :, :, pl.ds(u * 2 * LANES, 2 * LANES)] = jnp.zeros(
-                        (4 * nb, rows, 2 * LANES), F32
-                    )
+        pltpu.make_async_copy(held.at[slot], held.at[slot], loaded.at[slot]).wait()
+        partial[part] = matmul(left, held[slot]).reshape(4 * nb, rows, 2 * side_width)
 
         @pl.when(j + SLOTS < jobs)
         def _():
             load(j + SLOTS)
 
     def finish(j, kind, block, total):
-        for u in range(group):
-            gate = total[:, u * 2 * LANES: u * 2 * LANES + LANES]
-            up = total[:, u * 2 * LANES + LANES: (u + 1) * 2 * LANES]
-            column = pl.multiple_of((j * group + u) * LANES, LANES)
-            out[block, :, pl.ds(column, LANES)] = (
-                gate / (1.0 + jnp.exp(-gate)) * up
-            ).astype(BF16)
+        gate, up = total[:, :side_width], total[:, side_width:]
+        out[block, :, window(j * group, group)] = (
+            gate / (1.0 + jnp.exp(-gate)) * up
+        ).astype(BF16)
 
         @pl.when(j < kept_jobs)
         def _():
@@ -490,30 +496,25 @@
             kept[kind, :, pl.ds(pl.multiple_of(j * wide, LANES), wide)] = total
 
     def consume(j):
-        for u in range(group):
-            c = j * group + u
-            column = pl.multiple_of(c * LANES, LANES)
-            left = out[:, :, pl.ds(column, LANES)].reshape(members * height, LANES)
-
-            @pl.when(c < near_units)
-            def _(column=column, left=left):
-                turned[pl.ds(column, LANES), :] = left.T
-
-            for n in range(many - 1):
-                @pl.when((c >= starts[n]) & (c < starts[n + 1]))
-                def _(n=n, c=c, column=column, left=left):
-                    pl.when(c == starts[n])(lambda: near_copy(n).wait())
-                    total_of[n] += matmul(left, near[pl.ds(column, LANES), :])
-
-            @pl.when((c >= near_units) & (c < starts[-1]))
-            def _(c=c, left=left):
-                slot = lax.rem(c, below.shape[0])
-                below_copy(c).wait()
-                total_of[many - 1] += matmul(left, below[slot])
-
-                @pl.when(c + below.shape[0] < starts[-1])
-                def _():
-                    below_copy(c + below.shape[0]).start()
+        for n in range(many - 1):
+            pl.when(j == starts[n] // group)(lambda n=n: near_copy(n).wait())
+        for low, high, spans in cases:
+            @between(j, low, high)
+            def _(spans=spans):
+                for n, u, v in spans:
+                    here = window(j * group + u, v - u)
+                    left = out[:, :, here].reshape(members * height, (v - u) * LANES)
+                    if n < many - 1:
+                        turned[here, :] = left.T
+                        right = near[here, :]
+                    else:
+                        below_copy(j, u, v).wait()
+                        right = below[lax.rem(j, depth), pl.ds(u * LANES, (v - u) * LANES), :]
+                    total_of[n] += matmul(left, right)
+
+        @pl.when((j >= first_below) & (j + depth < jobs))
+        def _():
+            load_below(j + depth)
 
         @pl.when(j == near_job)
         def _():
@@ -554,14 +555,16 @@
     for spread in spreads:
         spread[2]()
     close_back = backward_relay(
-        dims_back, counts[:-1], full, near, kept, grads, partial_back, bufs_back, sems_back
+        dims_back, counts[:-1], group, full, near, kept, grads, partial_back, bufs_back,
+        sems_back,
     )
     for spread in spreads + [xs]:
         spread[3]()
     for n in range(many):
-        for p in range(pieces):
-            for k, (_, block, where) in enumerate(places):
-                share(n, p, k, block, where).wait_send()
+        for k, (_, block, where) in enumerate(places):
+            remote(
+                shares.at[n, block], got.at[k, n], ss.at[n, k], rs.at[0, n, k], where
+            ).wait_send()
     close()
     close_back()
 
@@ -575,8 +578,8 @@
     downs = [jnp.pad(d, ((0, -d.shape[0] % LANES), (0, 0))) for d in downs]
     counts = [w.shape[1] // LANES for w in weights[::2]]
     many = len(counts)
-    group = FORWARD_GROUP
-    jobs = -(-sum(counts) // group)
+    group = FORWARD_GROUP if sum(counts) % FORWARD_GROUP == 0 else 1
+    jobs = sum(counts) // group
     dims = (na, nb, jobs, min(jobs, ring_slots(na, FORWARD_STEPS)))
     kept_jobs = -(-(sum(counts[:-1]) + BACKWARD_GROUP - 1) // group)
     width = 2 * LANES * group
@@ -585,7 +588,7 @@
     hbm = pl.BlockSpec(memory_space=pltpu.HBM)
     dma = pltpu.SemaphoreType.DMA
     shape = jax.ShapeDtypeStruct
-    lower = 2 * group
+    lower = 3
     near_units = sum(counts[:-1])
     jobs_back = -(-near_units // BACKWARD_GROUP)
     dims_back = (na, nb, jobs_back, min(jobs_back, ring_slots(na, BACKWARD_STEPS)))
@@ -605,13 +608,13 @@
             pltpu.VMEM((4 * nb, rows, jobs * group * LANES), BF16),
             pltpu.VMEM((2, rows, kept_jobs * width), F32),
             pltpu.VMEM((near_units * LANES, features), BF16),
-            pltpu.VMEM((SLOTS, group, features, 2 * LANES), BF16), dma((SLOTS, group, 2)),
-            pltpu.VMEM((lower, LANES, features), BF16), dma((lower,)), dma((many - 1,)),
+            pltpu.VMEM((SLOTS, features, width), BF16), dma((SLOTS,)),
+            pltpu.VMEM((lower, group * LANES, features), BF16), dma((lower,)), dma((many - 1,)),
             pltpu.VMEM((many, tokens, features), F32),
             pltpu.VMEM((many, members, height, features), BF16),
             pltpu.VMEM((members - 1, many, height, features), BF16),
             dma((members - 1,)), dma((members - 1,)),
-            dma((pieces, many, members - 1)), dma((pieces, many, members - 1)),
+            dma((many, members - 1)), dma((pieces, many, members - 1)),
             dma((pieces, members - 1)), dma((pieces, members - 1)),
         ] + relay_scratch(dims, rows, width)
         + relay_scratch(dims_back, rows, BACKWARD_GROUP * LANES),
@@ -623,7 +626,7 @@
     return outs, counts
 
 
-def backward_relay(dims, counts, full, near, kept, out, partial, bufs, sems):
+def backward_relay(dims, counts, kept_group, full, near, kept, out, partial, bufs, sems):
     na, nb, jobs, slots = dims
     many = len(counts)
     group = BACKWARD_GROUP
@@ -631,30 +634,33 @@
     rows = out.shape[1]
     features = full.shape[3]
 
+    cases = cases_of(starts, group, jobs)
+
     def produce(j, part):
-        for u in range(group):
-            c = j * group + u
-            for n in range(many):
-                @pl.when((c >= starts[n]) & (c < starts[n + 1]))
-                def _(u=u, c=c, n=n):
+        for low, high, spans in cases:
+            @pl.when((j >= low) & (j < high))
+            def _(spans=spans):
+                for n, u, v in spans:
                     error = full[n].reshape(4 * nb * rows, features)
-                    row = pl.multiple_of(c * LANES, LANES)
-                    product = outer_cols(error, near[pl.ds(row, LANES), :])
-                    partial[part, :, :, pl.ds(u * LANES, LANES)] = product.reshape(
-                        4 * nb, rows, LANES
+                    row = pl.multiple_of((j * group + u) * LANES, LANES)
+                    product = outer_cols(error, near[pl.ds(row, (v - u) * LANES), :])
+                    partial[part, :, :, u * LANES: v * LANES] = product.reshape(
+                        4 * nb, rows, (v - u) * LANES
                     )
-
-            @pl.when(c >= starts[many])
-            def _(u=u):
-                partial[part, :, :, pl.ds(u * LANES, LANES)] = jnp.zeros(
-                    (4 * nb, rows, LANES), F32
-                )
+                last = spans[-1][2]
+                if last < group:
+                    partial[part, :, :, last * LANES:] = jnp.zeros(
+                        (4 * nb, rows, (group - last) * LANES), F32
+                    )
 
     def finish(j, kind, block, total):
         for u in range(group):
             column = pl.multiple_of((j * group + u) * 2 * LANES, LANES)
-            gate = kept[kind, :, pl.ds(column, LANES)]
-            up = kept[kind, :, pl.ds(column + LANES, LANES)]
+            c = j * group + u
+            where = c // kept_group * 2 * kept_group + lax.rem(c, kept_group)
+            where = pl.multiple_of(where * LANES, LANES)
+            gate = kept[kind, :, pl.ds(where, LANES)]
+            up = kept[kind, :, pl.ds(where + kept_group * LANES, LANES)]
             value = total[:, u * LANES: (u + 1) * LANES]
             s = 1.0 / (1.0 + jnp.exp(-gate))
             out[block, :, pl.ds(column, LANES)] = (
@@ -666,6 +672,21 @@
         dims, BACKWARD_STEPS, produce, finish, lambda j: None, partial, out,
         group * 2 * LANES, bufs, sems, None,
     )
+
+
+def cases_of(starts, group, jobs):
+    cases = []
+    for j in range(jobs):
+        spans = []
+        for n in range(len(starts) - 1):
+            low, high = max(starts[n], j * group), min(starts[n + 1], (j + 1) * group)
+            if low < high:
+                spans.append((n, low - j * group, high - j * group))
+        if cases and cases[-1][2] == spans:
+            cases[-1] = (cases[-1][0], j + 1, spans)
+        else:
+            cases.append((j, j + 1, spans))
+    return cases
 
 
 def padded(x):

time: 158 us -> 148 us (0.937)
  Pallas kernels: 157 us -> 146 us
    pallas_call x1, Pallas kernels: 148 us -> 137 us  [forward(): pl.pallas_call(functools.partial(step_kernel, dims, dims_back, counts, gr...]
where the time goes in v3:
time: 148 us
  Pallas kernels  146 us (99%)
    pallas_call x1, Pallas kernels, forward(): pl.pallas_call(functools.partial(step_kernel, dims, dims_back, counts, gr...  137 us
    pallas_call x1, Pallas kernels, weight_grads(): pl.pallas_call(functools.partial(outer_kernel, counts), grid=(features //...  8.82 us

profile of v3, /device:TPU:0, one launch (start us, length us, event | category | flops | bytes accessed | tf_op | source)
XLA Modules:
  0.0 147.8 jit_solution(7075177959665971527)
XLA Ops:
  0.6 0.0 copy-start
  0.7 0.8 copy-done
  1.5 137.4 %distill_step.1 = (bf16[4,32,1024]{2,1,0:T(8,128)(2,1)S(1)}, bf16[3200,128]{1,0:T(8,128)(2,1)S(1)}, bf16[32,1024]{1,0:T(8,128)(2,1)S(1)}, bf16[2,32,1024]{2,1,0:...) custom-call(bf16[32,1024]{1,0:T(8,128)(2,1)S(1)} %copy-done, ...), custom_call_target="tpu_custom_call" | custom-call | tf_op jit(solution)/shard_map/distill_step/pallas_call | solution.py:595
  138.9 8.8 %weight_grads.1 = (bf16[32,1024]{1,0:T(8,128)(2,1)}, bf16[32,1024]{1,0:T(8,128)(2,1)}, bf16[32,1024]{1,0:T(8,128)(2,1)}, bf16[1792,1024]{1,0:T(8,128)(2,1)}, bf1...) custom-call(bf16[128,1024]{1,0:T(8,128)(2,1)S(1)} %bitcast.3, ...), custom_call_target="tpu_custom_call" | custom-call | flops 2516582400 | bytes 19660800 | tf_op jit(solution)/shard_map/weight_grads/pallas_call | solution.py:729
Async XLA Ops:
  0.6 0.8 copy-start

commit v4 on v3

--- a/solution.py
+++ b/solution.py
@@ -16,6 +16,7 @@
 FORWARD_GROUP = 3
 BACKWARD_GROUP = 5
 STEP_MIB = 50
+GRAD_TILE = 256
 F32 = jnp.float32
 BF16 = jnp.bfloat16
 
@@ -90,9 +91,9 @@
         here = piece(a_block(lo, d), j)
         return remote(here, here, taz.at[d], uaz.at[j, d], back[d])
 
-    def spread_ay(j, d, k):
-        here = piece(a_block(lo, d), j)
-        return remote(here, here, tay.at[d, k], uay.at[j, d, k], beside[k])
+    def spread_ay(j, k):
+        here = piece(a_block(lo, 0), j, 2)
+        return remote(here, here, tay.at[k], uay.at[j, k], beside[k])
 
     def spread_by(j, k):
         here = piece(b_block(lo, turn), j)
@@ -153,8 +154,6 @@
         def _():
             finish(j, 0, a_block(lo, d), total)
             spread_az(j, d).start()
-            for k in range(side):
-                spread_ay(j, d, k).start()
 
     def along_b(j, d):
         slot = lax.rem(j, slots)
@@ -203,8 +202,10 @@
         def _():
             spread_az(j, d).start()
 
-        for k in range(side):
-            spread_ay(j, d, k).start()
+        @pl.when(far[d] > far[1 - d] - d)
+        def _():
+            for k in range(side):
+                spread_ay(j, k).start()
 
     def pass_b(j, d):
         spread_bz(j, d).wait_recv()
@@ -246,8 +247,7 @@
 
     def arrive(j):
         for k in range(side):
-            for d in range(2):
-                spread_ay(j, d, k).wait_recv()
+            spread_ay(j, k).wait_recv()
         consume(j)
 
     ready(0)
@@ -262,8 +262,7 @@
             remote(
                 ay_out.at[:, k], ay_in.at[:, k], say.at[k], ray.at[0, k], beside[k]
             ).wait_send()
-            for d in range(2):
-                spent(a_block(lo, d), 1, tay.at[d, k], uay.at[0, d, k], beside[k])
+            spent(a_block(lo, 0), 2, tay.at[k], uay.at[0, k], beside[k])
         for d in range(2):
             @pl.when(pos[d] < na - 1)
             def _(d=d):
@@ -302,7 +301,7 @@
         room(side, 2), room(side, 2), room(2), room(2),
         room(2, nb), room(2, nb), room(side), room(side),
     ]
-    counts = [(side,), (2,), (2,), (side,), (2, side), (2,), (2,), (side,)]
+    counts = [(side,), (2,), (2,), (side,), (side,), (2,), (2,), (side,)]
     sems = [dma(lead + c) for c in counts for lead in ((), (jobs,))]
     partial = pltpu.VMEM((slots, 4 * nb, rows, width), F32)
     return [partial] + bufs + sems
@@ -693,53 +692,83 @@
     return jnp.pad(x, ((0, 0), (0, -x.shape[1] % LANES)))
 
 
-def outer_kernel(counts, columns, grads, turned, full, target, own, *outs):
+def outer_kernel(counts, tile, columns, grads, turned, full, target, own, *refs):
     many = len(counts)
-    tokens = columns.shape[0]
-    outs[0][...] = target[...]
+    total = 1 + 4 * many
+    outs, stages, sems = refs[:total], refs[total: total + 3 * many], refs[-1]
+    tokens, features = columns.shape
+
+    def put(source, at):
+        return pltpu.make_async_copy(source, outs[at], sems.at[at])
+
+    put(target, 0).start()
     for n in range(many):
-        outs[1 + n][...] = own[n]
-    downs = outs[1 + many: 1 + 2 * many]
-    sides = outs[1 + 2 * many:]
-    left = columns[...].T
+        put(own.at[n], 1 + n).start()
+    ends = [(target, 0)] + [(own.at[n], 1 + n) for n in range(many)]
+
+    def part(n, at, start, size):
+        rows = pl.ds(start, size)
+        return pltpu.make_async_copy(
+            stages[n].at[rows, :], outs[at].at[rows, :], sems.at[at]
+        )
+
+    first = 1 + many
     c = 0
     for n, count in enumerate(counts):
-        gate, up = sides[2 * n], sides[2 * n + 1]
-        error = full[n].reshape(tokens, full.shape[3])
-        height = downs[n].shape[0]
-        at = c * LANES
-        downs[n][...] = matmul(turned[at: at + height, :], error).astype(BF16)
-        for u in range(count):
-            product = matmul(left, grads[:, c * 2 * LANES: (c + 1) * 2 * LANES]).astype(BF16)
-            size = min(LANES, gate.shape[1] - u * LANES)
-            gate[:, u * LANES: u * LANES + size] = product[:, :size]
-            up[:, u * LANES: u * LANES + size] = product[:, LANES: LANES + size]
-            c += 1
+        error = full[n].reshape(tokens, features)
+        height = outs[first + n].shape[0]
+        for start in range(0, height, tile):
+            size = min(tile, height - start)
+            at = c * LANES + start
+            stages[n][start: start + size, :] = matmul(
+                turned[at: at + size, :], error
+            ).astype(BF16)
+            part(n, first + n, start, size).start()
+        ends.append((stages[n], first + n))
+        c += count
+
+    def block(i, carry):
+        start = pl.multiple_of(i * tile, tile)
+        rows = pl.ds(start, tile)
+        left = columns[:, rows].T
+        c = 0
+        for n, count in enumerate(counts):
+            k = many + 2 * n
+            gate, up = stages[k], stages[k + 1]
+            for u in range(count):
+                product = matmul(left, grads[:, c * 2 * LANES: (c + 1) * 2 * LANES])
+                product = product.astype(BF16)
+                size = min(LANES, gate.shape[1] - u * LANES)
+                gate[rows, u * LANES: u * LANES + size] = product[:, :size]
+                up[rows, u * LANES: u * LANES + size] = product[:, LANES: LANES + size]
+                c += 1
+            part(k, first + k, start, tile).start()
+            part(k + 1, first + k + 1, start, tile).start()
+        return carry
+
+    lax.fori_loop(0, features // tile, block, 0)
+    for k in range(many, 3 * many):
+        ends.append((stages[k], first + k))
+    for source, at in ends:
+        put(source, at).wait()
 
 
 def weight_grads(columns, grads, turned, full, target, own, counts, widths):
     tokens, features = columns.shape
-    tile = 2 * LANES if features % (2 * LANES) == 0 else features
+    tile = GRAD_TILE if features % GRAD_TILE == 0 else features
     many, members, height = full.shape[:3]
     out_bytes = 6 * features * sum(widths)
-    sides = [w for w in widths for _ in range(2)]
     shape = jax.ShapeDtypeStruct
-    whole = pl.BlockSpec(memory_space=pltpu.VMEM)
-    lane = pl.BlockSpec((height, tile), lambda i: (0, i))
+    big = [(w, features) for w in widths] + [(features, w) for w in widths for _ in range(2)]
+    small = [(height, features)] * (1 + many)
+    vmem = pl.BlockSpec(memory_space=pltpu.VMEM)
     return pl.pallas_call(
-        functools.partial(outer_kernel, counts),
-        grid=(features // tile,),
-        out_shape=[shape((height, features), BF16)] * (1 + many)
-        + [shape((w, features), BF16) for w in widths]
-        + [shape((features, w), BF16) for w in sides],
-        in_specs=[
-            pl.BlockSpec((tokens, tile), lambda i: (0, i)), whole, whole,
-            pl.BlockSpec((many, members, height, tile), lambda i: (0, 0, 0, i)),
-            lane, pl.BlockSpec((many, height, tile), lambda i: (0, 0, i)),
-        ],
-        out_specs=[lane] * (1 + many)
-        + [pl.BlockSpec((w, tile), lambda i: (0, i)) for w in widths]
-        + [pl.BlockSpec((tile, w), lambda i: (i, 0)) for w in sides],
+        functools.partial(outer_kernel, counts, tile),
+        out_shape=[shape(x, BF16) for x in small + big],
+        in_specs=[vmem] * 6,
+        out_specs=[pl.BlockSpec(memory_space=pltpu.HBM)] * len(small + big),
+        scratch_shapes=[pltpu.VMEM(x, BF16) for x in big]
+        + [pltpu.SemaphoreType.DMA((len(small + big),))],
         compiler_params=pltpu.CompilerParams(vmem_limit_bytes=40 * MIB),
         cost_estimate=pl.CostEstimate(
             flops=tokens * out_bytes, bytes_accessed=out_bytes, transcendentals=0

time: 148 us -> 146 us (0.986)
  Pallas kernels: 146 us -> 144 us
where the time goes in v4:
time: 146 us
  Pallas kernels  144 us (99%)
    pallas_call x1, Pallas kernels, forward(): pl.pallas_call(functools.partial(step_kernel, dims, dims_back, counts, gr...  137 us
    pallas_call x1, Pallas kernels, weight_grads(): pl.pallas_call(functools.partial(outer_kernel, counts, tile), out_shape=[...  7.4 us

profile of v4, /device:TPU:0, one launch (start us, length us, event | category | flops | bytes accessed | tf_op | source)
XLA Modules:
  0.0 145.7 jit_solution(13673794205092053804)
XLA Ops:
  0.6 0.0 copy-start
  0.7 0.8 copy-done
  1.5 136.8 %distill_step.1 = (bf16[4,32,1024]{2,1,0:T(8,128)(2,1)S(1)}, bf16[3200,128]{1,0:T(8,128)(2,1)S(1)}, bf16[32,1024]{1,0:T(8,128)(2,1)S(1)}, bf16[2,32,1024]{2,1,0:...) custom-call(bf16[32,1024]{1,0:T(8,128)(2,1)S(1)} %copy-done, ...), custom_call_target="tpu_custom_call" | custom-call | tf_op jit(solution)/shard_map/distill_step/pallas_call | solution.py:594
  138.3 7.4 %weight_grads.1 = (bf16[32,1024]{1,0:T(8,128)(2,1)}, bf16[32,1024]{1,0:T(8,128)(2,1)}, bf16[32,1024]{1,0:T(8,128)(2,1)}, bf16[1792,1024]{1,0:T(8,128)(2,1)}, bf1...) custom-call(bf16[128,1024]{1,0:T(8,128)(2,1)S(1)} %bitcast.3, ...), custom_call_target="tpu_custom_call" | custom-call | flops 2516582400 | bytes 19660800 | tf_op jit(solution)/shard_map/weight_grads/pallas_call | solution.py:765
Async XLA Ops:
  0.6 0.8 copy-start

commit v5 on v4

--- a/solution.py
+++ b/solution.py
@@ -379,9 +379,9 @@
     (
         x, turned, target, own, full, grads, out, kept, near,
         held, loaded, below, lowered, stored, total_of, shares, got,
-        sx, rx, ss, rs, se, re,
-    ) = refs[1 + 3 * many: 24 + 3 * many]
-    rest = refs[24 + 3 * many:]
+        sx, rx, ss, rs, se, re, mine,
+    ) = refs[1 + 3 * many: 25 + 3 * many]
+    rest = refs[25 + 3 * many:]
     partial, bufs, sems = rest[0], rest[1:9], rest[9:25]
     partial_back, bufs_back, sems_back = rest[25], rest[26:34], rest[34:]
     starts = [sum(counts[:i]) for i in range(many + 1)]
@@ -439,7 +439,8 @@
             downs[n], near.at[pl.ds(starts[n] * LANES, height_n), :], stored.at[n]
         )
 
-    xs = spreader(sizes, lambda block: x.at[block], x_ref, (sx, rx))
+    xs = spreader(sizes, lambda block: x.at[block], None, (sx, rx))
+    x_own = pltpu.make_async_copy(x_ref, x.at[me], mine)
 
     def share(n, p, k, block, where):
         cols = pl.ds(p * step, step)
@@ -458,6 +459,7 @@
                 share(n, p, k, block, where).start()
 
     def prepare(barrier, count):
+        x_own.start()
         for _, _, where in places:
             pl.semaphore_signal(barrier, inc=1, device_id=where, device_id_type=MESH)
         for j in range(min(SLOTS, jobs)):
@@ -467,7 +469,7 @@
         for j in range(first_below, min(first_below + depth, jobs)):
             load_below(j)
         total_of[...] = jnp.zeros_like(total_of)
-        x[me] = x_ref[...]
+        x_own.wait()
         pl.semaphore_wait(barrier, count + len(places))
         xs[0]()
         xs[1]()
@@ -601,7 +603,7 @@
             shape((many - 1, members, height, features), BF16),
             shape((4 * nb, rows, jobs_back * BACKWARD_GROUP * 2 * LANES), BF16),
         ],
-        in_specs=[vmem] + [hbm] * (3 * many),
+        in_specs=[hbm] * (1 + 3 * many),
         out_specs=[vmem] * 6,
         scratch_shapes=[
             pltpu.VMEM((4 * nb, rows, jobs * group * LANES), BF16),
@@ -614,7 +616,7 @@
             pltpu.VMEM((members - 1, many, height, features), BF16),
             dma((members - 1,)), dma((members - 1,)),
             dma((many, members - 1)), dma((pieces, many, members - 1)),
-            dma((pieces, members - 1)), dma((pieces, members - 1)),
+            dma((pieces, members - 1)), dma((pieces, members - 1)), dma,
         ] + relay_scratch(dims, rows, width)
         + relay_scratch(dims_back, rows, BACKWARD_GROUP * LANES),
         compiler_params=pltpu.CompilerParams(
@@ -781,6 +783,7 @@
     tok, sizes, inputs, parent_gate, parent_up, parent_down, first_gate, first_up, first_down,
     second_gate, second_up, second_down,
 ):
+    inputs = pltpu.with_memory_space_constraint(inputs, pltpu.HBM)
     weights = (first_gate, first_up, second_gate, second_up, parent_gate, parent_up)
     downs = (first_down, second_down, parent_down)
     (x, turned, target, own, full, grads), counts = forward(

time: 146 us -> 145 us (level)
  no operation moved by 1% of the time
where the time goes in v5:
time: 145 us
  Pallas kernels  144 us (99%)
    pallas_call x1, Pallas kernels, forward(): pl.pallas_call(functools.partial(step_kernel, dims, dims_back, counts, gr...  137 us
    pallas_call x1, Pallas kernels, weight_grads(): pl.pallas_call(functools.partial(outer_kernel, counts, tile), out_shape=[...  7.41 us

profile of v5, /device:TPU:0, one launch (start us, length us, event | category | flops | bytes accessed | tf_op | source)
XLA Modules:
  0.0 144.8 jit_solution(17007464573460919113)
XLA Ops:
  0.6 136.8 %distill_step.1 = (bf16[4,32,1024]{2,1,0:T(8,128)(2,1)S(1)}, bf16[3200,128]{1,0:T(8,128)(2,1)S(1)}, bf16[32,1024]{1,0:T(8,128)(2,1)S(1)}, bf16[2,32,1024]{2,1,0:...) custom-call(bf16[32,1024]{1,0:T(8,128)(2,1)} %refs_0_.1, ...), custom_call_target="tpu_custom_call" | custom-call | tf_op jit(solution)/shard_map/distill_step/pallas_call | solution.py:596
  137.4 7.4 %weight_grads.1 = (bf16[32,1024]{1,0:T(8,128)(2,1)}, bf16[32,1024]{1,0:T(8,128)(2,1)}, bf16[32,1024]{1,0:T(8,128)(2,1)}, bf16[1792,1024]{1,0:T(8,128)(2,1)}, bf1...) custom-call(bf16[128,1024]{1,0:T(8,128)(2,1)S(1)} %bitcast.3, ...), custom_call_target="tpu_custom_call" | custom-call | flops 2516582400 | bytes 19660800 | tf_op jit(solution)/shard_map/weight_grads/pallas_call | solution.py:767
